TPU v7x, 256 devices: a whole 4x4x8 slice. The times are simulated.
256 devices in a mesh: tm: 64 (over z_lo, x, y, core), cell: 4 (over z_hi).
Axes of the slice: x: 4, y: 4, z: 8 (z_hi: 4, z_lo: 2; z = z_hi * 2 + z_lo), core: 2. Of those that a mesh axis runs over, the one named last changes fastest.
Arguments:
- theta: float32 [3, 1024, 256], P(None, 'cell', 'tm'), may hold values from -0.6 to 0.6
- tangent: float32 [3, 1024, 256], P(None, 'cell', 'tm'), may hold values from -6 to 6
- covariates: float32 [3, 2048, 32768], P(None, 'cell', 'tm'), may hold values from -4 to 4
- counts: int32 [2048, 32768], P('cell', 'tm'), may hold values from 0 to 5
- sfirst: int32 [2048], P('cell'), may hold values from 0 to 1008, as said below
- sweight: float32 [16, 2048], P(None, 'cell'), may hold values from 0.05 to 1
- tfirst: int32 [32768], P('tm'), may hold values from 0 to 252, as said below
- tweight: float32 [4, 32768], P(None, 'tm'), may hold values from 0.05 to 1
Outputs:
- hess_vec: float32 [3, 1024, 256], P(None, 'cell', 'tm')
- gradient: float32 [3, 1024, 256], P(None, 'cell', 'tm')
Inputs may be any that keep to these rules, and one draw needn't show every extreme that they name: Cell c's support block sfirst[c] to sfirst[c] + 15 lies within the basis functions (c // 512) * 256 - 16 to (c // 512 + 1) * 256 + 15. Hour h's support block tfirst[h] to tfirst[h] + 3 lies within the basis functions (h // 512) * 4 - 2 to (h // 512 + 1) * 4 + 1.
All inputs are finite; a program needn't handle non-finite values.
Results may differ from a plain program's by a relative error of at most 0.0002.
Values sent between devices are 32-bit elements; how exact they have to be, the bound alone decides.
No kernel may reach another device: no remote copies, remote signals or barrier semaphores. Data moves between devices by JAX's collectives and lax.ppermute only.
A program may use at most 64 MiB of HBM per device.

v0:
```python
import jax
import jax.numpy as jnp
from jax import lax
from jax.sharding import PartitionSpec as P

WS = 16
HS = 16
HT = 2


def with_halo(cells, sides, width):
    for axis, dim in sides:
        count = lax.axis_size(axis)
        ends = count - 1
        head = lax.slice_in_dim(cells, 0, width, axis=dim)
        tail = lax.slice_in_dim(cells, cells.shape[dim] - width, cells.shape[dim], axis=dim)
        cells = jnp.concatenate(
            [
                lax.ppermute(tail, axis, [(i, (i + 1) % count) for i in range(ends)]),
                cells,
                lax.ppermute(head, axis, [((i + 1) % count, i) for i in range(ends)]),
            ],
            axis=dim,
        )
    return cells


def from_behind(value, axis, steps):
    count = lax.axis_size(axis)
    first, last = (max(0, -steps), min(count, count - steps))
    return lax.ppermute(value, axis, [(source, source + steps) for source in range(first, last)])


def basis_block(first, values, row_total, offset):
    diffs = jnp.arange(row_total, dtype=jnp.int32)[:, None] - (first - offset)[None, :]
    result = jnp.zeros((row_total, first.shape[0]), jnp.float32)
    for index in range(values.shape[0]):
        result = result + jnp.where(diffs == index, values[index][None, :], jnp.float32(0.0))
    return result


def body(theta, tangent, covariates, counts, sfirst, sweight, tfirst, tweight):
    high = lax.Precision.HIGHEST
    row_count = theta.shape[1]
    col_count = theta.shape[2]
    hour_count = covariates.shape[2]
    stacked = jnp.stack([theta, tangent])
    widened = with_halo(stacked, (("tm", 3),), HT)
    col_start = lax.axis_index("tm") * col_count - HT
    extended = with_halo(widened, (("cell", 2),), HS)
    row_start = lax.axis_index("cell") * row_count - HS
    space_basis = basis_block(sfirst, sweight, row_count + 2 * HS, row_start)
    time_basis = basis_block(tfirst, tweight, widened.shape[3], col_start)
    spatial = jnp.einsum("sc,pkst->pkct", space_basis, extended, precision=high)
    fields = jnp.einsum("pkct,th->pkch", spatial, time_basis, precision=high)
    predictor = jnp.sum(covariates * fields[0], axis=0)
    tangent_pred = jnp.sum(covariates * fields[1], axis=0)
    rates = jnp.exp(predictor)
    weighted = jnp.stack(
        [
            covariates * (rates * tangent_pred)[None],
            covariates * (counts.astype(jnp.float32) - rates)[None],
        ]
    )
    time_part = jnp.einsum("pkch,th->pkct", weighted, time_basis, precision=high)
    col_pad = ((0, 0), (0, 0), (0, 0), (0, col_count - HT))
    col_pad_high = ((0, 0), (0, 0), (0, 0), (col_count - HT, 0))
    partial_value = jnp.einsum("sc,pkct->pkst", space_basis, time_part, precision=high)
    own_rows = partial_value[:, :, HS : HS + row_count]
    from_below = from_behind(partial_value[:, :, row_count + HS :], "cell", 1)
    from_above = from_behind(partial_value[:, :, :HS], "cell", -1)
    own_rows = own_rows + jnp.pad(from_below, ((0, 0), (0, 0), (0, row_count - HS), (0, 0)))
    own_rows = own_rows + jnp.pad(from_above, ((0, 0), (0, 0), (row_count - HS, 0), (0, 0)))
    middle = own_rows[..., HT : HT + col_count]
    cols_low = from_behind(own_rows[..., col_count + HT :], "tm", 1)
    cols_high = from_behind(own_rows[..., :HT], "tm", -1)
    summed = middle + jnp.pad(cols_low, col_pad) + jnp.pad(cols_high, col_pad_high)
    hess_vec = summed[0] / jnp.float32(WS * (hour_count // col_count))
    gradient = summed[1] / jnp.float32(hour_count // col_count)
    return (hess_vec, gradient)


def solution(mesh):
    return jax.shard_map(
        body,
        mesh=mesh,
        in_specs=(
            P(None, "cell", "tm"),
            P(None, "cell", "tm"),
            P(None, "cell", "tm"),
            P("cell", "tm"),
            P("cell"),
            P(None, "cell"),
            P("tm"),
            P(None, "tm"),
        ),
        out_specs=(P(None, "cell", "tm"), P(None, "cell", "tm")),
        check_vma=False,
    )
```

profile of v0, /device:TPU:31, one launch (start us, length us, event | category | flops | bytes accessed | tf_op | source)
XLA Modules:
  0.0 70.4 jit_solution(5553022456839844275)
XLA Ops:
  0.6 0.8 %fusion.46 = (f32[2,3,256,2]{2,3,1,0:T(2,128)S(1)}, f32[2,3,256,2]{2,3,1,0:T(2,128)S(1)}) fusion(f32[1,3,256,4]{2,3,1,0:T(4,128)} %bitcast.62, f32[1,3,256,4]{2,3,1,0:T(4,128)} %bitcast.65), kind=kLoop, calls=%fused_computation.63 | loop fusion | flops 6144 | bytes 49152 | tf_op jit(solution)/shard_map/stack | solution.py:47
  1.4 3.7 %collective-permute-start = (f32[2,3,256,2]{2,3,1,0:T(2,128)S(1)}, f32[2,3,256,2]{2,3,1,0:T(2,128)S(1)}, u32[]{:S(2)}, u32[]{:S(2)}) collective-permute-start(f32[2,3,256,2]{2,3,1,0:T(2,128)S(1)} %get-tuple-element.32), channel_id=1, source_target_pairs={{0,4},{4,8},{8,12},{12,16},{16,20},{20,24},{24,28},{28,32},{32,36}... | collective-permute-start | bytes 36872 | tf_op jit(solution)/shard_map/ppermute | solution.py:19
  5.1 1.9 %collective-permute-start.1 = (f32[2,3,256,2]{2,3,1,0:T(2,128)S(1)}, f32[2,3,256,2]{2,3,1,0:T(2,128)S(1)}, u32[]{:S(2)}, u32[]{:S(2)}) collective-permute-start(f32[2,3,256,2]{2,3,1,0:T(2,128)S(1)} %get-tuple-element.33), channel_id=1, source_target_pairs={{4,0},{8,4},{12,8},{16,12},{20,16},{24,20},{28,24},{32,28},{36,32}... | collective-permute-start | bytes 36872 | tf_op jit(solution)/shard_map/ppermute | solution.py:21
  7.1 0.9 %fusion.119 = (f32[1,512]{1,0:T(1,128)S(1)}, f32[1,512]{1,0:T(1,128)S(1)}, f32[1,512]{1,0:T(1,128)S(1)}, f32[1,512]{1,0:T(1,128)S(1)}) fusion(f32[4,512]{1,0:T(4,128)} %param.15), kind=kLoop, calls=%fused_computation.141 | loop fusion | bytes 16384 | tf_op jit(solution)/shard_map/slice | solution.py:38
  7.9 1.1 %fusion.118 = (f32[1,512]{1,0:T(1,128)S(1)}, f32[1,512]{1,0:T(1,128)S(1)}, f32[1,512]{1,0:T(1,128)S(1)}, f32[1,512]{1,0:T(1,128)S(1)}, f32[1,512]{1,0:T(1,128)S(...) fusion(f32[16,512]{1,0:T(8,128)} %param.13), kind=kLoop, calls=%fused_computation.140 | loop fusion | bytes 65536 | tf_op jit(solution)/shard_map/slice | solution.py:38
  9.0 0.7 broadcast_subtract_fusion.1
  9.7 0.0 collective-permute-done
  9.7 4.7 %collective-permute-done.1 = f32[2,3,256,2]{2,3,1,0:T(2,128)S(1)} collective-permute-done((f32[2,3,256,2]{2,3,1,0:T(2,128)S(1)}, f32[2,3,256,2]{2,3,1,0:T(2,128)S(1)}, u32[]{:S(2)}, u32[]{:S(2)}) %collective-permute-start.1) | collective-permute-done | bytes 12320 | tf_op jit(solution)/shard_map/ppermute | solution.py:21
  14.4 0.7 %pad_maximum_fusion = f32[2,3,256,8]{2,3,1,0:T(8,128)S(1)} fusion(f32[2,3,256,2]{2,3,1,0:T(2,128)S(1)} %collective-permute-done.1, f32[1,3,256,4]{2,3,1,0:T(4,128)} %bitcast.66, f32[1,3,256,4]{2,3,1,0:T(4,128)} %bitcast.63, f32[2,3,256,2]{2,3,1,0:T(2,128)S(1)} %collective-permute-done), kind=kLoop, calls=%fused_computation.49 | loop fusion | flops 36864 | bytes 98304 | tf_op jit(solution)/shard_map/concatenate | solution.py:17
  15.1 0.1 fusion.117
  15.2 4.9 %collective-permute-start.2 = (f32[2,3,16,8]{2,3,1,0:T(8,128)S(1)}, f32[2,3,16,8]{2,3,1,0:T(8,128)S(1)}, u32[]{:S(2)}, u32[]{:S(2)}) collective-permute-start(f32[2,3,16,8]{2,3,1,0:T(8,128)S(1)} %get-tuple-element.12), channel_id=1, source_target_pairs={{0,1},{1,2},{2,3},{4,5},{5,6},{6,7},{8,9},{9,10},{10,11},{12,13},{... | collective-permute-start | bytes 9224 | tf_op jit(solution)/shard_map/ppermute | solution.py:19
  20.1 1.3 %collective-permute-start.3 = (f32[2,3,16,8]{2,3,1,0:T(8,128)S(1)}, f32[2,3,16,8]{2,3,1,0:T(8,128)S(1)}, u32[]{:S(2)}, u32[]{:S(2)}) collective-permute-start(f32[2,3,16,8]{2,3,1,0:T(8,128)S(1)} %get-tuple-element.13), channel_id=1, source_target_pairs={{1,0},{2,1},{3,2},{5,4},{6,5},{7,6},{9,8},{10,9},{11,10},{13,12},{... | collective-permute-start | bytes 9224 | tf_op jit(solution)/shard_map/ppermute | solution.py:21
  21.4 0.7 broadcast_subtract_fusion
  22.1 4.4 %collective-permute-done.3 = f32[2,3,16,8]{2,3,1,0:T(8,128)S(1)} collective-permute-done((f32[2,3,16,8]{2,3,1,0:T(8,128)S(1)}, f32[2,3,16,8]{2,3,1,0:T(8,128)S(1)}, u32[]{:S(2)}, u32[]{:S(2)}) %collective-permute-start.3) | collective-permute-done | bytes 3104 | tf_op jit(solution)/shard_map/ppermute | solution.py:21
  26.5 2.2 %convolution_bitcast_fusion = f32[2,3,512,8]{2,3,1,0:T(8,128)S(1)} fusion(f32[512]{0:T(512)S(1)} %bitcast.104, f32[512]{0:T(512)S(1)} %bitcast.106, f32[512]{0:T(512)S(1)} %bitcast.78, f32[512]{0:T(512)S(1)} %bitcast.80, f32[512]{0:T(512)S(1)} %bitcast.82, f32[512]{0:T(512)S(1)} %bitcast.84, f32[512]{0:T(512)S(1)} %bitcast.86, f32[512]{0:T(512)S(1)} %bitcast.88, ...), kind=kOutput, calls=%fused_computation.12 | convolution fusion | flops 92081664 | bytes 188416 | tf_op jit(solution)/shard_map/sc,pkst->pkct/dot_general | solution.py:54
  28.7 0.0 copy-start
  28.7 5.1 %fusion.40 = f32[2,3,512,512]{3,2,1,0:T(8,128)S(1)} fusion(f32[2,3,512,8]{2,3,1,0:T(8,128)S(1)} %convolution_bitcast_fusion, f32[512]{0:T(512)S(1)} %bitcast.72, f32[512]{0:T(512)S(1)} %bitcast.74, f32[512]{0:T(512)S(1)} %bitcast.70, f32[512]{0:T(512)S(1)} %bitcast.68, s32[512]{0:T(512)S(1)} %broadcast_subtract_fusion), kind=kOutput, calls=%fused_computation.55 | convolution fusion | flops 151044096 | bytes 6400000 | tf_op jit(solution)/shard_map/pkct,th->pkch/dot_general | solution.py:55
  33.8 0.0 copy-start.1
  33.8 1.3 %fusion.5 = (f32[512,512]{1,0:T(8,128)S(1)}, f32[512,512]{1,0:T(8,128)S(1)}) fusion(f32[3,512,512]{2,1,0:T(8,128)S(1)} %copy-done, f32[2,3,512,512]{3,2,1,0:T(8,128)S(1)} %fusion.40), kind=kLoop, calls=%fused_computation.6 | loop fusion | flops 2621440 | bytes 11534336 | tf_op jit(solution)/shard_map/reduce_sum | solution.py:57
  35.2 0.4 exponential_multiply_fusion
  35.5 0.9 %multiply_bitcast_fusion.1 = (f32[1,3,512,512]{3,2,1,0:T(8,128)S(1)}, f32[1,3,512,512]{3,2,1,0:T(8,128)S(1)}) fusion(f32[3,512,512]{2,1,0:T(8,128)S(1)} %copy-done, f32[512,512]{1,0:T(8,128)S(1)} %get-tuple-element.6, f32[512,512]{1,0:T(8,128)S(1)} %get-tuple-element.7), kind=kLoop, calls=%fused_computation.11 | loop fusion | flops 1572864 | bytes 11534336 | tf_op jit(solution)/shard_map/stack | solution.py:59
  36.4 5.3 %fusion = f32[2,3,512,8]{2,3,1,0:T(8,128)S(1)} fusion(f32[1,3,512,512]{3,2,1,0:T(8,128)S(1)} %get-tuple-element.5, f32[1,3,512,512]{3,2,1,0:T(8,128)S(1)} %get-tuple-element.4, f32[512]{0:T(512)S(1)} %bitcast.73, f32[512]{0:T(512)S(1)} %bitcast.75, f32[512]{0:T(512)S(1)} %bitcast.71, f32[512]{0:T(512)S(1)} %bitcast.69, s32[512]{0:T(512)S(1)} %broadcast_subtract_fusion), kind=kOutput, calls=%fused_computation | convolution fusion | flops 152616960 | bytes 6400000 | tf_op jit(solution)/shard_map/pkch,th->pkct/dot_general | solution.py:65
  41.7 1.6 %convolution_bitcast_fusion.1 = f32[2,3,288,8]{2,3,1,0:T(8,128)S(1)} fusion(f32[2,3,512,8]{2,3,1,0:T(8,128)S(1)} %fusion, f32[512]{0:T(512)S(1)} %bitcast.105, f32[512]{0:T(512)S(1)} %bitcast.107, f32[512]{0:T(512)S(1)} %bitcast.79, f32[512]{0:T(512)S(1)} %bitcast.81, f32[512]{0:T(512)S(1)} %bitcast.83, f32[512]{0:T(512)S(1)} %bitcast.85, ...), kind=kOutput, calls=%fused_computation.13 | convolution fusion | flops 92012544 | bytes 188416 | tf_op jit(solution)/shard_map/sc,pkct->pkst/dot_general | solution.py:68
  43.3 0.1 fusion.115
  43.4 5.4 %collective-permute-start.4 = (f32[2,3,16,8]{2,3,1,0:T(8,128)S(1)}, f32[2,3,16,8]{2,3,1,0:T(8,128)S(1)}, u32[]{:S(2)}, u32[]{:S(2)}) collective-permute-start(f32[2,3,16,8]{2,3,1,0:T(8,128)S(1)} %get-tuple-element.8), channel_id=1, source_target_pairs={{0,1},{1,2},{2,3},{4,5},{5,6},{6,7},{8,9},{9,10},{10,11},{12,13},{... | collective-permute-start | bytes 9224 | tf_op jit(solution)/shard_map/ppermute | solution.py:31
  48.8 1.3 %collective-permute-start.5 = (f32[2,3,16,8]{2,3,1,0:T(8,128)S(1)}, f32[2,3,16,8]{2,3,1,0:T(8,128)S(1)}, u32[]{:S(2)}, u32[]{:S(2)}) collective-permute-start(f32[2,3,16,8]{2,3,1,0:T(8,128)S(1)} %get-tuple-element.9), channel_id=1, source_target_pairs={{1,0},{2,1},{3,2},{5,4},{6,5},{7,6},{9,8},{10,9},{11,10},{13,12},{... | collective-permute-start | bytes 9224 | tf_op jit(solution)/shard_map/ppermute | solution.py:31
  50.2 4.2 %collective-permute-done.5 = f32[2,3,16,8]{2,3,1,0:T(8,128)S(1)} collective-permute-done((f32[2,3,16,8]{2,3,1,0:T(8,128)S(1)}, f32[2,3,16,8]{2,3,1,0:T(8,128)S(1)}, u32[]{:S(2)}, u32[]{:S(2)}) %collective-permute-start.5) | collective-permute-done | bytes 3104 | tf_op jit(solution)/shard_map/ppermute | solution.py:31
  54.3 0.1 fusion.37
  54.4 6.1 %collective-permute-start.6 = (f32[2,3,256,2]{2,3,1,0:T(2,128)S(1)}, f32[2,3,256,2]{2,3,1,0:T(2,128)S(1)}, u32[]{:S(2)}, u32[]{:S(2)}) collective-permute-start(f32[2,3,256,2]{2,3,1,0:T(2,128)S(1)} %get-tuple-element.10), channel_id=1, source_target_pairs={{0,4},{4,8},{8,12},{12,16},{16,20},{20,24},{24,28},{28,32},{32,36}... | collective-permute-start | bytes 36872 | tf_op jit(solution)/shard_map/ppermute | solution.py:31
  60.5 1.9 %collective-permute-start.7 = (f32[2,3,256,2]{2,3,1,0:T(2,128)S(1)}, f32[2,3,256,2]{2,3,1,0:T(2,128)S(1)}, u32[]{:S(2)}, u32[]{:S(2)}) collective-permute-start(f32[2,3,256,2]{2,3,1,0:T(2,128)S(1)} %get-tuple-element.11), channel_id=1, source_target_pairs={{4,0},{8,4},{12,8},{16,12},{20,16},{24,20},{28,24},{32,28},{36,32}... | collective-permute-start | bytes 36872 | tf_op jit(solution)/shard_map/ppermute | solution.py:31
  62.5 7.3 %collective-permute-done.7 = f32[2,3,256,2]{2,3,1,0:T(2,128)S(1)} collective-permute-done((f32[2,3,256,2]{2,3,1,0:T(2,128)S(1)}, f32[2,3,256,2]{2,3,1,0:T(2,128)S(1)}, u32[]{:S(2)}, u32[]{:S(2)}) %collective-permute-start.7) | collective-permute-done | bytes 12320 | tf_op jit(solution)/shard_map/ppermute | solution.py:31
  69.8 0.6 fusion.47
  (7 shorter events, 0.0 us)
Async XLA Ops:
  1.4 8.3 %collective-permute-start = (f32[2,3,256,2]{2,3,1,0:T(2,128)S(1)}, f32[2,3,256,2]{2,3,1,0:T(2,128)S(1)}, u32[]{:S(2)}, u32[]{:S(2)}) collective-permute-start(f32[2,3,256,2]{2,3,1,0:T(2,128)S(1)} %get-tuple-element.32), channel_id=1, source_target_pairs={{0,4},{4,8},{8,12},{12,16},{16,20},{20,24},{24,28},{28,32},{32,36}... | collective-permute-start | bytes 36872 | tf_op jit(solution)/shard_map/ppermute | solution.py:19
  5.1 9.2 %collective-permute-start.1 = (f32[2,3,256,2]{2,3,1,0:T(2,128)S(1)}, f32[2,3,256,2]{2,3,1,0:T(2,128)S(1)}, u32[]{:S(2)}, u32[]{:S(2)}) collective-permute-start(f32[2,3,256,2]{2,3,1,0:T(2,128)S(1)} %get-tuple-element.33), channel_id=1, source_target_pairs={{4,0},{8,4},{12,8},{16,12},{20,16},{24,20},{28,24},{32,28},{36,32}... | collective-permute-start | bytes 36872 | tf_op jit(solution)/shard_map/ppermute | solution.py:21
  15.2 6.9 %collective-permute-start.2 = (f32[2,3,16,8]{2,3,1,0:T(8,128)S(1)}, f32[2,3,16,8]{2,3,1,0:T(8,128)S(1)}, u32[]{:S(2)}, u32[]{:S(2)}) collective-permute-start(f32[2,3,16,8]{2,3,1,0:T(8,128)S(1)} %get-tuple-element.12), channel_id=1, source_target_pairs={{0,1},{1,2},{2,3},{4,5},{5,6},{6,7},{8,9},{9,10},{10,11},{12,13},{... | collective-permute-start | bytes 9224 | tf_op jit(solution)/shard_map/ppermute | solution.py:19
  20.1 6.4 %collective-permute-start.3 = (f32[2,3,16,8]{2,3,1,0:T(8,128)S(1)}, f32[2,3,16,8]{2,3,1,0:T(8,128)S(1)}, u32[]{:S(2)}, u32[]{:S(2)}) collective-permute-start(f32[2,3,16,8]{2,3,1,0:T(8,128)S(1)} %get-tuple-element.13), channel_id=1, source_target_pairs={{1,0},{2,1},{3,2},{5,4},{6,5},{7,6},{9,8},{10,9},{11,10},{13,12},{... | collective-permute-start | bytes 9224 | tf_op jit(solution)/shard_map/ppermute | solution.py:21
  28.7 5.1 %copy-start = (f32[3,512,512]{2,1,0:T(8,128)S(1)}, f32[3,512,512]{2,1,0:T(8,128)}, u32[]{:S(2)}) copy-start(f32[3,512,512]{2,1,0:T(8,128)} %param.10) | copy-start | bytes 9437188
  33.8 1.3 %copy-start.1 = (s32[512,512]{1,0:T(8,128)S(1)}, s32[512,512]{1,0:T(8,128)}, u32[]{:S(2)}) copy-start(s32[512,512]{1,0:T(8,128)} %param.11) | copy-start | bytes 3145732
  43.4 6.8 %collective-permute-start.4 = (f32[2,3,16,8]{2,3,1,0:T(8,128)S(1)}, f32[2,3,16,8]{2,3,1,0:T(8,128)S(1)}, u32[]{:S(2)}, u32[]{:S(2)}) collective-permute-start(f32[2,3,16,8]{2,3,1,0:T(8,128)S(1)} %get-tuple-element.8), channel_id=1, source_target_pairs={{0,1},{1,2},{2,3},{4,5},{5,6},{6,7},{8,9},{9,10},{10,11},{12,13},{... | collective-permute-start | bytes 9224 | tf_op jit(solution)/shard_map/ppermute | solution.py:31
  48.8 5.5 %collective-permute-start.5 = (f32[2,3,16,8]{2,3,1,0:T(8,128)S(1)}, f32[2,3,16,8]{2,3,1,0:T(8,128)S(1)}, u32[]{:S(2)}, u32[]{:S(2)}) collective-permute-start(f32[2,3,16,8]{2,3,1,0:T(8,128)S(1)} %get-tuple-element.9), channel_id=1, source_target_pairs={{1,0},{2,1},{3,2},{5,4},{6,5},{7,6},{9,8},{10,9},{11,10},{13,12},{... | collective-permute-start | bytes 9224 | tf_op jit(solution)/shard_map/ppermute | solution.py:31
  54.4 8.0 %collective-permute-start.6 = (f32[2,3,256,2]{2,3,1,0:T(2,128)S(1)}, f32[2,3,256,2]{2,3,1,0:T(2,128)S(1)}, u32[]{:S(2)}, u32[]{:S(2)}) collective-permute-start(f32[2,3,256,2]{2,3,1,0:T(2,128)S(1)} %get-tuple-element.10), channel_id=1, source_target_pairs={{0,4},{4,8},{8,12},{12,16},{16,20},{20,24},{24,28},{28,32},{32,36}... | collective-permute-start | bytes 36872 | tf_op jit(solution)/shard_map/ppermute | solution.py:31
  60.5 9.2 %collective-permute-start.7 = (f32[2,3,256,2]{2,3,1,0:T(2,128)S(1)}, f32[2,3,256,2]{2,3,1,0:T(2,128)S(1)}, u32[]{:S(2)}, u32[]{:S(2)}) collective-permute-start(f32[2,3,256,2]{2,3,1,0:T(2,128)S(1)} %get-tuple-element.11), channel_id=1, source_target_pairs={{4,0},{8,4},{12,8},{16,12},{20,16},{24,20},{28,24},{32,28},{36,32}... | collective-permute-start | bytes 36872 | tf_op jit(solution)/shard_map/ppermute | solution.py:31
where the time goes:
time: 71.3 us; the launch traced here: 70.4 us
  starting transfers between devices  26.5 us (37%)
  waiting for transfers between devices  20.6 us (29%)
  matrix products  14.2 us (20%)
  other arithmetic  6.19 us (9%)
  local copies, waits for them, and re-layouts  2.11 us (3%)
  between operations  0.83 us (1%)
    ppermute x4, starting transfers between devices, from_behind(): lax.ppermute(value, axis, [(source, source + steps) for source in range(f...  14.7 us
    ppermute x4, waiting for transfers between devices, from_behind(): lax.ppermute(value, axis, [(source, source + steps) for source in range(f...  11.5 us
    ppermute x2, waiting for transfers between devices, with_halo(): lax.ppermute(head, axis, [((i + 1) % count, i) for i in range(ends)])  9.09 us
    ppermute x2, starting transfers between devices, with_halo(): lax.ppermute(tail, axis, [(i, (i + 1) % count) for i in range(ends)])  8.57 us
    dot_general x1, matrix products, body(): jnp.einsum('pkch,th->pkct', weighted, time_basis, precision=high)  5.3 us
    dot_general x1, matrix products, body(): fields = jnp.einsum('pkct,th->pkch', spatial, time_basis, precision=high)  5.1 us
    ppermute x2, starting transfers between devices, with_halo(): lax.ppermute(head, axis, [((i + 1) % count, i) for i in range(ends)])  3.21 us
    dot_general x1, matrix products, body(): spatial = jnp.einsum('sc,pkst->pkct', space_basis, extended, precision=high)  2.21 us
  transfers between devices with their start and end apart: 8, of which 4 were waited for; matrix products, arithmetic and copies ran while one was open for 5% of the time, Pallas kernels for 0%

commit v1 on v0

v1 whole, which is shorter than its diff:
```python
import jax
import jax.numpy as jnp
from jax import lax
from jax.experimental import pallas as pl
from jax.experimental.pallas import tpu as pltpu
from jax.sharding import PartitionSpec as P

HS = 16
HT = 2
F32 = jnp.float32
BF16 = jnp.bfloat16
VMEM = pl.BlockSpec(memory_space=pltpu.VMEM)


def split(x):
    high = x.astype(BF16)
    return high, (x - high.astype(F32)).astype(BF16)


def iota(shape, dim):
    return lax.broadcasted_iota(jnp.int32, shape, dim)


def dot(a, b):
    return jnp.dot(a, b, preferred_element_type=F32)


def parity(axis):
    return lax.rem(lax.axis_index(axis), 2)


def edges_kernel(theta_ref, tangent_ref, near_ref, far_ref):
    odd = parity("tm") == 1
    for p, ref in enumerate((theta_ref, tangent_ref)):
        for k in range(3):
            rows = pl.ds(2 * (3 * p + k), 2)
            low, high = ref[k, 0:HT, :], ref[k, HT : 2 * HT, :]
            near_ref[rows, :] = jnp.where(odd, low, high)
            far_ref[rows, :] = jnp.where(odd, high, low)


def widen_kernel(theta_ref, tangent_ref, near_ref, far_ref, coef_ref, one_ref, two_ref, wide):
    odd = parity("tm") == 1
    wide[...] = jnp.zeros_like(wide)
    for p, ref in enumerate((theta_ref, tangent_ref)):
        for k in range(3):
            pk = 3 * p + k
            near, far = near_ref[2 * pk : 2 * pk + 2, :], far_ref[2 * pk : 2 * pk + 2, :]
            for base in (0, 64):
                wide[base + 8 * pk : base + 8 * pk + 2, :] = jnp.where(odd, near, far)
                wide[base + 8 * pk + 2 : base + 8 * pk + 6, :] = ref[k]
                wide[base + 8 * pk + 6 : base + 8 * pk + 8, :] = jnp.where(odd, far, near)
    turned = wide[...].T
    coef_ref[...] = turned
    low, high = turned[0:HS], turned[turned.shape[0] - HS :]
    below = parity("cell") == 1
    one_ref[...] = jnp.where(below, low, high)
    two_ref[...] = jnp.where(below, high, low)


def prepare_kernel(
    coef_ref, sfirst_ref, sweight_ref, tfirst_ref, tweight_ref, shigh_ref, slow_ref, edge_ref, spread_ref, gather_ref, main_ref
):
    rows = coef_ref.shape[0]
    offset = lax.axis_index("cell") * rows - HS
    first = sfirst_ref[...] - offset
    cells = first.shape[1]
    blocks = []
    for start in range(0, rows + 2 * HS, 32):
        diffs = iota((32, cells), 0) + start - first
        total = jnp.zeros((32, cells), F32)
        for index in range(sweight_ref.shape[0]):
            total = jnp.where(diffs == index, sweight_ref[index : index + 1, :], total)
        high, low = split(total)
        shigh_ref[start : start + 32, :] = high
        slow_ref[start : start + 32, :] = low
        blocks.append(total)
    space = jnp.concatenate(blocks, axis=0)
    own_high, own_low = split(space[HS : HS + rows].T)
    edge = jnp.concatenate([space[:HS], space[HS + rows :]], axis=0)
    edge_all = jnp.concatenate([edge, edge, edge, jnp.zeros_like(edge)], axis=0).T
    edge_high, edge_low = split(edge_all)
    part = iota(edge_all.shape, 1) // 32
    edge_ref[...] = jnp.where(part == 1, edge_low.astype(F32), edge_high.astype(F32)).astype(BF16)
    coef_high, coef_low = split(coef_ref[...])
    main_ref[...] = dot(own_high, coef_high) + dot(own_low, coef_high) + dot(own_high, coef_low)

    tfirst = tfirst_ref[...] - (lax.axis_index("tm") * 4 - HT)
    hours = tfirst.shape[1]
    row = iota((192, hours), 0)
    diffs = row % 8 - tfirst
    total = jnp.zeros((192, hours), F32)
    for index in range(tweight_ref.shape[0]):
        total = jnp.where(diffs == index, tweight_ref[index : index + 1, :], total)
    high, low = split(total)
    high, low = high.astype(F32), low.astype(F32)
    spread = jnp.where(row < 128, high, low)
    owner = (row // 8) % 8
    turned = jnp.where(row[:128] < 64, high[:128], low[:128]).T
    lane = (iota(turned.shape, 1) // 8) % 8
    for pk in range(6):
        mine = jnp.where(owner == pk, spread, 0.0).astype(BF16)
        back = jnp.where(lane == pk, turned, 0.0).astype(BF16)
        for j in range(4):
            spread_ref[j, :, 128 * pk : 128 * pk + 128] = mine[:, 128 * j : 128 * j + 128]
            gather_ref[j, 128 * pk : 128 * pk + 128, :] = back[128 * j : 128 * j + 128, :]


def main_kernel(
    main_ref, one_ref, two_ref, edge_ref, spread_ref, gather_ref, shigh_ref, slow_ref, cov_ref, counts_ref,
    own_ref, send_one_ref, send_two_ref, fields, whigh, wlow,
):
    odd = parity("cell") == 1
    one, two = one_ref[...], two_ref[...]
    halo = jnp.concatenate([jnp.where(odd, one, two), jnp.where(odd, two, one)], axis=0)
    halo_high, halo_low = split(halo)
    stacked = jnp.concatenate([halo_high, halo_high, halo_low, jnp.zeros_like(halo_low)], axis=0)
    spatial = main_ref[...] + dot(edge_ref[...], stacked)
    high = spatial.astype(BF16).astype(F32)
    left = iota(spatial.shape, 1) < 64
    factor = jnp.concatenate(
        [jnp.where(left, high, spatial - high).astype(BF16), jnp.where(left, high, 0.0).astype(BF16)[:, :64]], axis=1
    )

    def forward(j):
        fields[j] = dot(factor, spread_ref[j])

    def weigh(j):
        lanes = slice(128 * j, 128 * j + 128)
        for start in range(0, fields.shape[1], 16):
            rows = slice(start, start + 16)
            cov = [cov_ref[k, rows, lanes] for k in range(3)]
            at = [fields[j, rows, 128 * pk : 128 * pk + 128] for pk in range(6)]
            rates = jnp.exp(cov[0] * at[0] + cov[1] * at[1] + cov[2] * at[2])
            slope = rates * (cov[0] * at[3] + cov[1] * at[4] + cov[2] * at[5])
            excess = counts_ref[rows, lanes].astype(F32) - rates
            for p, value in enumerate((slope, excess)):
                for k in range(3):
                    columns = slice(128 * (3 * p + k), 128 * (3 * p + k) + 128)
                    upper, lower = split(cov[k] * value)
                    whigh[j, rows, columns] = upper
                    wlow[j, rows, columns] = lower

    def back(j):
        return dot(whigh[j], gather_ref[j]) + dot(wlow[j], gather_ref[j])

    forward(0)
    total = jnp.zeros(spatial.shape, F32)
    for j in range(4):
        if j < 3:
            forward(j + 1)
        weigh(j)
        if j > 0:
            total = total + back(j - 1)
    total = total + back(3)
    total = total + pltpu.roll(total, 64, 1)
    total_high, total_low = split(total)
    summed = dot(shigh_ref[...], total_high) + dot(slow_ref[...], total_high) + dot(shigh_ref[...], total_low)
    count = own_ref.shape[0]
    own_ref[...] = summed[HS : HS + count]
    low, high = summed[:HS], summed[HS + count :]
    send_one_ref[...] = jnp.where(odd, low, high)
    send_two_ref[...] = jnp.where(odd, high, low)


def turn_kernel(own_ref, one_ref, two_ref, wide_ref, near_ref, far_ref):
    below = parity("cell") == 1
    one, two = one_ref[...], two_ref[...]
    count = own_ref.shape[0]
    low = own_ref[:HS] + jnp.where(below, one, two)
    high = own_ref[count - HS :] + jnp.where(below, two, one)
    turned = jnp.concatenate([low, own_ref[HS : count - HS], high], axis=0).T
    wide_ref[...] = turned[:48]
    odd = parity("tm") == 1
    for pk in range(6):
        low, high = turned[8 * pk : 8 * pk + 2], turned[8 * pk + 6 : 8 * pk + 8]
        near_ref[2 * pk : 2 * pk + 2, :] = jnp.where(odd, low, high)
        far_ref[2 * pk : 2 * pk + 2, :] = jnp.where(odd, high, low)


def finish_kernel(wide_ref, near_ref, far_ref, hess_ref, grad_ref, *, scales):
    odd = parity("tm") == 1
    for p, ref in enumerate((hess_ref, grad_ref)):
        for k in range(3):
            pk = 3 * p + k
            near, far = near_ref[2 * pk : 2 * pk + 2, :], far_ref[2 * pk : 2 * pk + 2, :]
            ref[k, 0:2, :] = (wide_ref[8 * pk + 2 : 8 * pk + 4, :] + jnp.where(odd, near, far)) * scales[p]
            ref[k, 2:4, :] = (wide_ref[8 * pk + 4 : 8 * pk + 6, :] + jnp.where(odd, far, near)) * scales[p]


def call(kernel, outs, scratch=(), **kwargs):
    return pl.pallas_call(
        kernel,
        out_shape=tuple(jax.ShapeDtypeStruct(s, d) for s, d in outs),
        out_specs=tuple(VMEM for _ in outs),
        scratch_shapes=list(scratch),
        **kwargs,
    )


def swap(value, axis, pairs):
    return lax.ppermute(value, axis, [(a, b) for a, b in pairs] + [(b, a) for a, b in pairs])


def body(theta, tangent, covariates, counts, sfirst, sweight, tfirst, tweight):
    hours = counts.shape[1]
    rows = theta.shape[1]
    cells = counts.shape[0]
    periods, regions = lax.axis_size("tm"), lax.axis_size("cell")

    def over_tm(near, far):
        return (
            swap(near, "tm", [(t, t + 1) for t in range(0, periods, 2)]),
            swap(far, "tm", [(t, t + 1) for t in range(1, periods - 1, 2)]),
        )

    def over_cell(one, two):
        second = swap(two, "cell", [(c, c + 1) for c in range(1, regions - 1, 2)])
        return swap(one, "cell", [(c, c + 1) for c in range(0, regions, 2)]), second

    theta_t, tangent_t = jnp.swapaxes(theta, 1, 2), jnp.swapaxes(tangent, 1, 2)
    strip = ((12, rows), F32)
    band = ((HS, 128), F32)
    near, far = over_tm(*call(edges_kernel, [strip, strip])(theta_t, tangent_t))
    coef, one, two = call(widen_kernel, [((rows, 128), F32), band, band], [pltpu.VMEM((128, rows), F32)])(
        theta_t, tangent_t, near, far
    )
    one, two = over_cell(one, two)
    span = rows + 2 * HS
    shigh, slow, edge, spread, gather, main = call(
        prepare_kernel,
        [
            ((span, cells), BF16), ((span, cells), BF16), ((cells, 128), BF16),
            ((4, 192, 768), BF16), ((4, 768, 128), BF16), ((cells, 128), F32),
        ],
    )(coef, sfirst[None], sweight, tfirst[None], tweight)
    own, one, two = call(
        main_kernel,
        [((rows, 128), F32), band, band],
        [pltpu.VMEM((4, cells, 768), F32), pltpu.VMEM((4, cells, 768), BF16), pltpu.VMEM((4, cells, 768), BF16)],
    )(main, one, two, edge, spread, gather, shigh, slow, covariates, counts)
    one, two = over_cell(one, two)
    wide, near, far = call(turn_kernel, [((48, rows), F32), strip, strip])(own, one, two)
    near, far = over_tm(near, far)
    scales = (1.0 / (16 * (hours // 4)), 1.0 / (hours // 4))

    def last(*refs):
        finish_kernel(*refs, scales=scales)

    hess, grad = call(last, [((3, 4, rows), F32)] * 2)(wide, near, far)
    return jnp.swapaxes(hess, 1, 2), jnp.swapaxes(grad, 1, 2)


def solution(mesh):
    return jax.shard_map(
        body,
        mesh=mesh,
        in_specs=(
            P(None, "cell", "tm"),
            P(None, "cell", "tm"),
            P(None, "cell", "tm"),
            P("cell", "tm"),
            P("cell"),
            P(None, "cell"),
            P("tm"),
            P(None, "tm"),
        ),
        out_specs=(P(None, "cell", "tm"), P(None, "cell", "tm")),
        check_vma=False,
    )
```

time: 71.3 us -> 55.3 us (0.78)
  the two profiles are of different devices: /device:TPU:31 before, /device:TPU:96 now
where the time goes in v1:
time: 55.3 us; the launch traced here: 54.8 us
  starting transfers between devices  24 us (43%)
  Pallas kernels  17.9 us (32%)
  waiting for transfers between devices  9.72 us (18%)
  local copies, waits for them, and re-layouts  2.39 us (4%)
  between operations  0.73 us (1%)
    ppermute x8, starting transfers between devices, swap(): lax.ppermute(value, axis, [(a, b) for a, b in pairs] + [(b, a) for a, b i...  24 us
    ppermute x8, waiting for transfers between devices, swap(): lax.ppermute(value, axis, [(a, b) for a, b in pairs] + [(b, a) for a, b i...  9.72 us
    pallas_call x1, Pallas kernels, body(): call(main_kernel, [((rows, 128), F32), band, band], [pltpu.VMEM((4, cells...  8.43 us
    pallas_call x1, Pallas kernels, body(): call(prepare_kernel, [((span, cells), BF16), ((span, cells), BF16), ((cel...  3.51 us
    unnamed x16, local copies, waits for them, and re-layouts  2.39 us
    pallas_call x1, Pallas kernels, body(): call(turn_kernel, [((48, rows), F32), strip, strip])(own, one, two)  1.66 us
    pallas_call x1, Pallas kernels, body(): call(widen_kernel, [((rows, 128), F32), band, band], [pltpu.VMEM((128, ro...  1.55 us
    pallas_call x1, Pallas kernels, body(): hess, grad = call(last, [((3, 4, rows), F32)] * 2)(wide, near, far)  1.44 us
  transfers between devices with their start and end apart: 8, of which 4 were waited for; matrix products, arithmetic and copies ran while one was open for 0% of the time, Pallas kernels for 6%

profile of v1, /device:TPU:96, one launch (start us, length us, event | category | flops | bytes accessed | tf_op | source)
XLA Modules:
  0.0 54.8 jit_solution(16300345347128021253)
XLA Ops:
  0.6 1.3 %shard_map.95 = (f32[12,256]{1,0:T(8,128)}, f32[12,256]{1,0:T(8,128)}) custom-call(f32[3,4,256]{2,1,0:T(4,128)} %bitcast.6, f32[3,4,256]{2,1,0:T(4,128)} %bitcast.8), custom_call_target="tpu_custom_call" | custom-call | tf_op jit(solution)/shard_map/pallas_call | solution.py:224
  2.0 0.0 collective-permute-start
  2.0 6.8 %collective-permute-start.1 = (f32[12,256]{1,0:T(8,128)}, f32[12,256]{1,0:T(8,128)S(1)}, u32[]{:S(2)}, u32[]{:S(2)}) collective-permute-start(f32[12,256]{1,0:T(8,128)} %get-tuple-element.22), channel_id=1, source_target_pairs={{4,8},{12,16},{20,24},{28,32},{36,40},{44,48},{52,56},{60,64},{68,... | collective-permute-start | bytes 36872 | tf_op jit(solution)/shard_map/ppermute | solution.py:202
  8.8 0.0 collective-permute-done.near_ref
  8.8 0.0 copy-start
  8.8 2.7 %collective-permute-done.1.far_ref = f32[12,256]{1,0:T(8,128)S(1)} collective-permute-done((f32[12,256]{1,0:T(8,128)}, f32[12,256]{1,0:T(8,128)S(1)}, u32[]{:S(2)}, u32[]{:S(2)}) %collective-permute-start.1) | collective-permute-done | bytes 12320 | tf_op jit(solution)/shard_map/ppermute | solution.py:202
  11.5 0.0 copy-done
  11.5 0.6 %copy-done.3 = f32[12,256]{1,0:T(8,128)} copy-done((f32[12,256]{1,0:T(8,128)}, f32[12,256]{1,0:T(8,128)S(1)}, u32[]{:S(2)}) %copy-start.3) | copy-done | bytes 12312
  12.1 1.5 %shard_map.96 = (f32[256,128]{1,0:T(8,128)}, f32[16,128]{1,0:T(8,128)}, f32[16,128]{1,0:T(8,128)}) custom-call(f32[3,4,256]{2,1,0:T(4,128)} %bitcast.7, f32[3,4,256]{2,1,0:T(4,128)} %bitcast.9, f32[12,256]{1,0:T(8,128)} %copy-done, f32[12,256]{1,0:T(8,128)} %copy-done.3), custom_call_target="tpu_custom_call" | custom-call | tf_op jit(solution)/shard_map/pallas_call | solution.py:225
  13.6 0.0 collective-permute-start.2
  13.6 6.9 %collective-permute-start.3 = (f32[16,128]{1,0:T(8,128)}, f32[16,128]{1,0:T(8,128)S(1)}, u32[]{:S(2)}, u32[]{:S(2)}) collective-permute-start(f32[16,128]{1,0:T(8,128)} %get-tuple-element.26), channel_id=1, source_target_pairs={{1,2},{2,1},{5,6},{6,5},{9,10},{10,9},{13,14},{14,13},{17,18},{18,... | collective-permute-start | bytes 24584 | tf_op jit(solution)/shard_map/ppermute | solution.py:202
  20.6 3.5 %shard_map.97 = (bf16[288,512]{1,0:T(8,128)(2,1)}, bf16[288,512]{1,0:T(8,128)(2,1)}, bf16[512,128]{1,0:T(8,128)(2,1)}, bf16[4,192,768]{2,1,0:T(8,128)(2,1)}, bf1...) custom-call(f32[256,128]{1,0:T(8,128)} %get-tuple-element.23.coef_ref, s32[1,512]{1,0:T(1,128)} %bitcast.10, ...), custom_call_target="tpu_custom_call" | custom-call | tf_op jit(solution)/shard_map/pallas_call | solution.py:230
  24.1 0.0 collective-permute-done.2.one_ref
  24.1 0.0 collective-permute-done.3.two_ref
  24.1 0.0 copy-start.5
  24.1 0.6 %copy-done.4 = f32[16,128]{1,0:T(8,128)} copy-done((f32[16,128]{1,0:T(8,128)}, f32[16,128]{1,0:T(8,128)S(1)}, u32[]{:S(2)}) %copy-start.4) | copy-done | bytes 8216
  24.7 0.0 copy-done.5
  24.7 8.4 %shard_map.98 = (f32[256,128]{1,0:T(8,128)}, f32[16,128]{1,0:T(8,128)}, f32[16,128]{1,0:T(8,128)}) custom-call(f32[512,128]{1,0:T(8,128)} %get-tuple-element.24.main_ref, f32[16,128]{1,0:T(8,128)} %copy-done.4, f32[16,128]{1,0:T(8,128)} %copy-done.5, bf16[512,128]{1,0:T(8,128)(2,1)} %get-tuple-element.27.edge_ref, ...), custom_call_target="tpu_custom_call" | custom-call | tf_op jit(solution)/shard_map/pallas_call | solution.py:237
  33.1 0.0 collective-permute-start.4
  33.1 4.3 %collective-permute-start.5 = (f32[16,128]{1,0:T(8,128)}, f32[16,128]{1,0:T(8,128)S(1)}, u32[]{:S(2)}, u32[]{:S(2)}) collective-permute-start(f32[16,128]{1,0:T(8,128)} %get-tuple-element.34), channel_id=1, source_target_pairs={{1,2},{2,1},{5,6},{6,5},{9,10},{10,9},{13,14},{14,13},{17,18},{18,... | collective-permute-start | bytes 24584 | tf_op jit(solution)/shard_map/ppermute | solution.py:202
  37.5 0.4 collective-permute-done.4.one_ref
  37.9 3.1 %collective-permute-done.5.two_ref = f32[16,128]{1,0:T(8,128)S(1)} collective-permute-done((f32[16,128]{1,0:T(8,128)}, f32[16,128]{1,0:T(8,128)S(1)}, u32[]{:S(2)}, u32[]{:S(2)}) %collective-permute-start.5) | collective-permute-done | bytes 8224 | tf_op jit(solution)/shard_map/ppermute | solution.py:202
  41.0 0.0 copy-done.6
  41.0 0.6 %copy-done.7 = f32[16,128]{1,0:T(8,128)} copy-done((f32[16,128]{1,0:T(8,128)}, f32[16,128]{1,0:T(8,128)S(1)}, u32[]{:S(2)}) %copy-start.7) | copy-done | bytes 8216
  41.6 1.7 %shard_map.99 = (f32[48,256]{1,0:T(8,128)}, f32[12,256]{1,0:T(8,128)}, f32[12,256]{1,0:T(8,128)}) custom-call(f32[256,128]{1,0:T(8,128)} %get-tuple-element.32.own_ref, f32[16,128]{1,0:T(8,128)} %copy-done.6, f32[16,128]{1,0:T(8,128)} %copy-done.7), custom_call_target="tpu_custom_call" | custom-call | tf_op jit(solution)/shard_map/pallas_call | solution.py:243
  43.3 0.0 collective-permute-start.6
  43.3 6.0 %collective-permute-start.7 = (f32[12,256]{1,0:T(8,128)}, f32[12,256]{1,0:T(8,128)S(1)}, u32[]{:S(2)}, u32[]{:S(2)}) collective-permute-start(f32[12,256]{1,0:T(8,128)} %get-tuple-element.37), channel_id=1, source_target_pairs={{4,8},{12,16},{20,24},{28,32},{36,40},{44,48},{52,56},{60,64},{68,... | collective-permute-start | bytes 36872 | tf_op jit(solution)/shard_map/ppermute | solution.py:202
  49.2 0.0 collective-permute-done.6.refs_1_
  49.2 0.0 copy-start.1
  49.2 3.5 %collective-permute-done.7.refs_2_ = f32[12,256]{1,0:T(8,128)S(1)} collective-permute-done((f32[12,256]{1,0:T(8,128)}, f32[12,256]{1,0:T(8,128)S(1)}, u32[]{:S(2)}, u32[]{:S(2)}) %collective-permute-start.7) | collective-permute-done | bytes 12320 | tf_op jit(solution)/shard_map/ppermute | solution.py:202
  52.7 0.6 %copy-done.2 = f32[12,256]{1,0:T(8,128)} copy-done((f32[12,256]{1,0:T(8,128)}, f32[12,256]{1,0:T(8,128)S(1)}, u32[]{:S(2)}) %copy-start.2) | copy-done | bytes 12312
  53.3 1.4 %shard_map.100 = (f32[3,4,256]{2,1,0:T(4,128)}, f32[3,4,256]{2,1,0:T(4,128)}) custom-call(f32[48,256]{1,0:T(8,128)} %get-tuple-element.35.refs_0_, f32[12,256]{1,0:T(8,128)} %copy-done.1, f32[12,256]{1,0:T(8,128)} %copy-done.2), custom_call_target="tpu_custom_call" | custom-call | tf_op jit(solution)/shard_map/pallas_call | solution.py:250
  (6 shorter events, 0.0 us)
Async XLA Ops:
  2.0 6.8 %collective-permute-start = (f32[12,256]{1,0:T(8,128)}, f32[12,256]{1,0:T(8,128)S(1)}, u32[]{:S(2)}, u32[]{:S(2)}) collective-permute-start(f32[12,256]{1,0:T(8,128)} %get-tuple-element.21), channel_id=1, source_target_pairs={{0,4},{8,12},{16,20},{24,28},{32,36},{40,44},{48,52},{56,60},{64,6... | collective-permute-start | bytes 36872 | tf_op jit(solution)/shard_map/ppermute | solution.py:202
  2.0 9.5 %collective-permute-start.1 = (f32[12,256]{1,0:T(8,128)}, f32[12,256]{1,0:T(8,128)S(1)}, u32[]{:S(2)}, u32[]{:S(2)}) collective-permute-start(f32[12,256]{1,0:T(8,128)} %get-tuple-element.22), channel_id=1, source_target_pairs={{4,8},{12,16},{20,24},{28,32},{36,40},{44,48},{52,56},{60,64},{68,... | collective-permute-start | bytes 36872 | tf_op jit(solution)/shard_map/ppermute | solution.py:202
  8.8 2.7 %copy-start = (f32[12,256]{1,0:T(8,128)}, f32[12,256]{1,0:T(8,128)S(1)}, u32[]{:S(2)}) copy-start(f32[12,256]{1,0:T(8,128)S(1)} %collective-permute-done.near_ref) | copy-start | bytes 36868
  11.5 0.6 %copy-start.3 = (f32[12,256]{1,0:T(8,128)}, f32[12,256]{1,0:T(8,128)S(1)}, u32[]{:S(2)}) copy-start(f32[12,256]{1,0:T(8,128)S(1)} %collective-permute-done.1.far_ref) | copy-start | bytes 36868
  13.6 10.5 %collective-permute-start.2 = (f32[16,128]{1,0:T(8,128)}, f32[16,128]{1,0:T(8,128)S(1)}, u32[]{:S(2)}, u32[]{:S(2)}) collective-permute-start(f32[16,128]{1,0:T(8,128)} %get-tuple-element.25), channel_id=1, source_target_pairs={{0,1},{2,3},{1,0},{3,2},{4,5},{6,7},{5,4},{7,6},{8,9},{10,11},{9,8... | collective-permute-start | bytes 24584 | tf_op jit(solution)/shard_map/ppermute | solution.py:202
  13.6 10.5 %collective-permute-start.3 = (f32[16,128]{1,0:T(8,128)}, f32[16,128]{1,0:T(8,128)S(1)}, u32[]{:S(2)}, u32[]{:S(2)}) collective-permute-start(f32[16,128]{1,0:T(8,128)} %get-tuple-element.26), channel_id=1, source_target_pairs={{1,2},{2,1},{5,6},{6,5},{9,10},{10,9},{13,14},{14,13},{17,18},{18,... | collective-permute-start | bytes 24584 | tf_op jit(solution)/shard_map/ppermute | solution.py:202
  24.1 0.6 %copy-start.4 = (f32[16,128]{1,0:T(8,128)}, f32[16,128]{1,0:T(8,128)S(1)}, u32[]{:S(2)}) copy-start(f32[16,128]{1,0:T(8,128)S(1)} %collective-permute-done.2.one_ref) | copy-start | bytes 24580
  24.1 0.6 %copy-start.5 = (f32[16,128]{1,0:T(8,128)}, f32[16,128]{1,0:T(8,128)S(1)}, u32[]{:S(2)}) copy-start(f32[16,128]{1,0:T(8,128)S(1)} %collective-permute-done.3.two_ref) | copy-start | bytes 24580
  33.1 4.8 %collective-permute-start.4 = (f32[16,128]{1,0:T(8,128)}, f32[16,128]{1,0:T(8,128)S(1)}, u32[]{:S(2)}, u32[]{:S(2)}) collective-permute-start(f32[16,128]{1,0:T(8,128)} %get-tuple-element.33), channel_id=1, source_target_pairs={{0,1},{2,3},{1,0},{3,2},{4,5},{6,7},{5,4},{7,6},{8,9},{10,11},{9,8... | collective-permute-start | bytes 24584 | tf_op jit(solution)/shard_map/ppermute | solution.py:202
  33.1 7.9 %collective-permute-start.5 = (f32[16,128]{1,0:T(8,128)}, f32[16,128]{1,0:T(8,128)S(1)}, u32[]{:S(2)}, u32[]{:S(2)}) collective-permute-start(f32[16,128]{1,0:T(8,128)} %get-tuple-element.34), channel_id=1, source_target_pairs={{1,2},{2,1},{5,6},{6,5},{9,10},{10,9},{13,14},{14,13},{17,18},{18,... | collective-permute-start | bytes 24584 | tf_op jit(solution)/shard_map/ppermute | solution.py:202
  37.9 3.1 %copy-start.6 = (f32[16,128]{1,0:T(8,128)}, f32[16,128]{1,0:T(8,128)S(1)}, u32[]{:S(2)}) copy-start(f32[16,128]{1,0:T(8,128)S(1)} %collective-permute-done.4.one_ref) | copy-start | bytes 24580
  41.0 0.6 %copy-start.7 = (f32[16,128]{1,0:T(8,128)}, f32[16,128]{1,0:T(8,128)S(1)}, u32[]{:S(2)}) copy-start(f32[16,128]{1,0:T(8,128)S(1)} %collective-permute-done.5.two_ref) | copy-start | bytes 24580
  43.3 6.0 %collective-permute-start.6 = (f32[12,256]{1,0:T(8,128)}, f32[12,256]{1,0:T(8,128)S(1)}, u32[]{:S(2)}, u32[]{:S(2)}) collective-permute-start(f32[12,256]{1,0:T(8,128)} %get-tuple-element.36), channel_id=1, source_target_pairs={{0,4},{8,12},{16,20},{24,28},{32,36},{40,44},{48,52},{56,60},{64,6... | collective-permute-start | bytes 36872 | tf_op jit(solution)/shard_map/ppermute | solution.py:202
  43.3 9.5 %collective-permute-start.7 = (f32[12,256]{1,0:T(8,128)}, f32[12,256]{1,0:T(8,128)S(1)}, u32[]{:S(2)}, u32[]{:S(2)}) collective-permute-start(f32[12,256]{1,0:T(8,128)} %get-tuple-element.37), channel_id=1, source_target_pairs={{4,8},{12,16},{20,24},{28,32},{36,40},{44,48},{52,56},{60,64},{68,... | collective-permute-start | bytes 36872 | tf_op jit(solution)/shard_map/ppermute | solution.py:202
  49.2 3.5 %copy-start.1 = (f32[12,256]{1,0:T(8,128)}, f32[12,256]{1,0:T(8,128)S(1)}, u32[]{:S(2)}) copy-start(f32[12,256]{1,0:T(8,128)S(1)} %collective-permute-done.6.refs_1_) | copy-start | bytes 36868
  52.7 0.6 %copy-start.2 = (f32[12,256]{1,0:T(8,128)}, f32[12,256]{1,0:T(8,128)S(1)}, u32[]{:S(2)}) copy-start(f32[12,256]{1,0:T(8,128)S(1)} %collective-permute-done.7.refs_2_) | copy-start | bytes 36868

commit v2 on v1

--- a/solution.py
+++ b/solution.py
@@ -29,9 +29,15 @@
     return lax.rem(lax.axis_index(axis), 2)
 
 
-def edges_kernel(theta_ref, tangent_ref, near_ref, far_ref):
-    odd = parity("tm") == 1
-    for p, ref in enumerate((theta_ref, tangent_ref)):
+def load_kernel(*refs):
+    sources, held, (near_ref, far_ref, sems) = refs[:6], refs[6:12], refs[12:]
+    copies = [pltpu.make_async_copy(a, b, sems.at[i]) for i, (a, b) in enumerate(zip(sources, held))]
+    for copy in copies:
+        copy.start()
+    for copy in copies:
+        copy.wait()
+    odd = parity("tm") == 1
+    for p, ref in enumerate(held[:2]):
         for k in range(3):
             rows = pl.ds(2 * (3 * p + k), 2)
             low, high = ref[k, 0:HT, :], ref[k, HT : 2 * HT, :]
@@ -39,7 +45,7 @@
             far_ref[rows, :] = jnp.where(odd, high, low)
 
 
-def widen_kernel(theta_ref, tangent_ref, near_ref, far_ref, coef_ref, one_ref, two_ref, wide):
+def widen_kernel(theta_ref, tangent_ref, near_ref, far_ref, after_ref, coef_ref, one_ref, two_ref, wide):
     odd = parity("tm") == 1
     wide[...] = jnp.zeros_like(wide)
     for p, ref in enumerate((theta_ref, tangent_ref)):
@@ -58,10 +64,14 @@
     two_ref[...] = jnp.where(below, high, low)
 
 
-def prepare_kernel(
-    coef_ref, sfirst_ref, sweight_ref, tfirst_ref, tweight_ref, shigh_ref, slow_ref, edge_ref, spread_ref, gather_ref, main_ref
+def basis_kernel(
+    sfirst_ref, sweight_ref, tfirst_ref, tweight_ref, cov_any, counts_any,
+    shigh_ref, slow_ref, turned_high_ref, turned_low_ref, edge_ref, spread_ref, gather_ref, cov_ref, counts_ref, sems,
 ):
-    rows = coef_ref.shape[0]
+    copies = (pltpu.make_async_copy(cov_any, cov_ref, sems.at[0]), pltpu.make_async_copy(counts_any, counts_ref, sems.at[1]))
+    for copy in copies:
+        copy.start()
+    rows = turned_high_ref.shape[1]
     offset = lax.axis_index("cell") * rows - HS
     first = sfirst_ref[...] - offset
     cells = first.shape[1]
@@ -76,14 +86,12 @@
         slow_ref[start : start + 32, :] = low
         blocks.append(total)
     space = jnp.concatenate(blocks, axis=0)
-    own_high, own_low = split(space[HS : HS + rows].T)
+    turned_high_ref[...], turned_low_ref[...] = split(space[HS : HS + rows].T)
     edge = jnp.concatenate([space[:HS], space[HS + rows :]], axis=0)
     edge_all = jnp.concatenate([edge, edge, edge, jnp.zeros_like(edge)], axis=0).T
     edge_high, edge_low = split(edge_all)
     part = iota(edge_all.shape, 1) // 32
     edge_ref[...] = jnp.where(part == 1, edge_low.astype(F32), edge_high.astype(F32)).astype(BF16)
-    coef_high, coef_low = split(coef_ref[...])
-    main_ref[...] = dot(own_high, coef_high) + dot(own_low, coef_high) + dot(own_high, coef_low)
 
     tfirst = tfirst_ref[...] - (lax.axis_index("tm") * 4 - HT)
     hours = tfirst.shape[1]
@@ -104,6 +112,13 @@
         for j in range(4):
             spread_ref[j, :, 128 * pk : 128 * pk + 128] = mine[:, 128 * j : 128 * j + 128]
             gather_ref[j, 128 * pk : 128 * pk + 128, :] = back[128 * j : 128 * j + 128, :]
+    for copy in copies:
+        copy.wait()
+
+
+def inner_kernel(coef_ref, high_ref, low_ref, main_ref):
+    coef_high, coef_low = split(coef_ref[...])
+    main_ref[...] = dot(high_ref[...], coef_high) + dot(low_ref[...], coef_high) + dot(high_ref[...], coef_low)
 
 
 def main_kernel(
@@ -188,14 +203,21 @@
             ref[k, 2:4, :] = (wide_ref[8 * pk + 4 : 8 * pk + 6, :] + jnp.where(odd, far, near)) * scales[p]
 
 
-def call(kernel, outs, scratch=(), **kwargs):
-    return pl.pallas_call(
-        kernel,
-        out_shape=tuple(jax.ShapeDtypeStruct(s, d) for s, d in outs),
-        out_specs=tuple(VMEM for _ in outs),
-        scratch_shapes=list(scratch),
-        **kwargs,
-    )
+def call(kernel, outs, scratch=(), final=False, apart=()):
+    shape = jax.ShapeDtypeStruct if final else pltpu.VMEM
+
+    def run(*args):
+        places = [pl.BlockSpec(memory_space=pltpu.HBM) if i in apart else VMEM for i in range(len(args))]
+        return pl.pallas_call(
+            kernel,
+            out_shape=tuple(shape(s, d) for s, d in outs),
+            in_specs=places,
+            out_specs=tuple(VMEM for _ in outs),
+            scratch_shapes=list(scratch),
+            compiler_params=pltpu.CompilerParams(vmem_limit_bytes=24 << 20),
+        )(*(pltpu.with_memory_space_constraint(a, pltpu.HBM if i in apart else pltpu.VMEM) for i, a in enumerate(args)))
+
+    return run
 
 
 def swap(value, axis, pairs):
@@ -218,22 +240,28 @@
         second = swap(two, "cell", [(c, c + 1) for c in range(1, regions - 1, 2)])
         return swap(one, "cell", [(c, c + 1) for c in range(0, regions, 2)]), second
 
-    theta_t, tangent_t = jnp.swapaxes(theta, 1, 2), jnp.swapaxes(tangent, 1, 2)
+    small = (jnp.swapaxes(theta, 1, 2), jnp.swapaxes(tangent, 1, 2), sfirst[None], sweight, tfirst[None], tweight)
     strip = ((12, rows), F32)
     band = ((HS, 128), F32)
-    near, far = over_tm(*call(edges_kernel, [strip, strip])(theta_t, tangent_t))
+    theta_t, tangent_t, *support, near, far = call(
+        load_kernel, [(a.shape, a.dtype) for a in small] + [strip, strip], [pltpu.SemaphoreType.DMA((6,))], apart=range(6)
+    )(*small)
+    near, far = over_tm(near, far)
+    span = rows + 2 * HS
+    shigh, slow, turned_high, turned_low, edge, spread, gather, covariates, counts = call(
+        basis_kernel,
+        [
+            ((span, cells), BF16), ((span, cells), BF16), ((cells, rows), BF16), ((cells, rows), BF16), ((cells, 128), BF16),
+            ((4, 192, 768), BF16), ((4, 768, 128), BF16), (covariates.shape, F32), (counts.shape, counts.dtype),
+        ],
+        [pltpu.SemaphoreType.DMA((2,))],
+        apart=(4, 5),
+    )(*support, covariates, counts)
     coef, one, two = call(widen_kernel, [((rows, 128), F32), band, band], [pltpu.VMEM((128, rows), F32)])(
-        theta_t, tangent_t, near, far
+        theta_t, tangent_t, near, far, edge
     )
     one, two = over_cell(one, two)
-    span = rows + 2 * HS
-    shigh, slow, edge, spread, gather, main = call(
-        prepare_kernel,
-        [
-            ((span, cells), BF16), ((span, cells), BF16), ((cells, 128), BF16),
-            ((4, 192, 768), BF16), ((4, 768, 128), BF16), ((cells, 128), F32),
-        ],
-    )(coef, sfirst[None], sweight, tfirst[None], tweight)
+    (main,) = call(inner_kernel, [((cells, 128), F32)])(coef, turned_high, turned_low)
     own, one, two = call(
         main_kernel,
         [((rows, 128), F32), band, band],
@@ -247,7 +275,7 @@
     def last(*refs):
         finish_kernel(*refs, scales=scales)
 
-    hess, grad = call(last, [((3, 4, rows), F32)] * 2)(wide, near, far)
+    hess, grad = call(last, [((3, 4, rows), F32)] * 2, final=True)(wide, near, far)
     return jnp.swapaxes(hess, 1, 2), jnp.swapaxes(grad, 1, 2)
 
 

time: 55.3 us -> 43.9 us (0.79)
  Pallas kernels: 17.9 us -> 9.18 us
  local copies, waits for them, and re-layouts: 2.39 us -> 0 us
  waiting for transfers between devices: 9.72 us -> 7.66 us
  starting transfers between devices: 24 us -> 25.4 us
    pallas_call x6 -> x7, Pallas kernels: 17.9 us -> 9.18 us  [run(): pl.pallas_call(kernel, out_shape=tuple((shape(s, d) for s, d in outs)), i...]
    unnamed x16 -> x0, local copies, waits for them, and re-layouts: 2.39 us -> none
    ppermute x8, waiting for transfers between devices: 9.72 us -> 7.66 us  [swap(): lax.ppermute(value, axis, [(a, b) for a, b in pairs] + [(b, a) for a, b i...]
    ppermute x8, starting transfers between devices: 24 us -> 25.4 us  [swap(): lax.ppermute(value, axis, [(a, b) for a, b in pairs] + [(b, a) for a, b i...]
where the time goes in v2:
time: 43.9 us; the launch traced here: 43.1 us
  starting transfers between devices  25.4 us (58%)
  Pallas kernels  9.18 us (21%)
  waiting for transfers between devices  7.66 us (17%)
  between operations  0.77 us (2%)
    ppermute x8, starting transfers between devices, swap(): lax.ppermute(value, axis, [(a, b) for a, b in pairs] + [(b, a) for a, b i...  25.4 us
    pallas_call x7, Pallas kernels, run(): pl.pallas_call(kernel, out_shape=tuple((shape(s, d) for s, d in outs)), i...  9.18 us
    ppermute x8, waiting for transfers between devices, swap(): lax.ppermute(value, axis, [(a, b) for a, b in pairs] + [(b, a) for a, b i...  7.66 us
  transfers between devices with their start and end apart: 8, of which 4 were waited for; matrix products, arithmetic and copies ran while one was open for 0% of the time, Pallas kernels for 6%

profile of v2, /device:TPU:96, one launch (start us, length us, event | category | flops | bytes accessed | tf_op | source)
XLA Modules:
  0.0 43.1 jit_solution(18220140403126317906)
XLA Ops:
  0.6 0.9 %shard_map.95 = (f32[3,4,256]{2,1,0:T(4,128)S(1)}, f32[3,4,256]{2,1,0:T(4,128)S(1)}, s32[1,512]{1,0:T(1,128)S(1)}, f32[16,512]{1,0:T(8,128)S(1)}, s32[1,512]{1,0...) custom-call(f32[3,4,256]{2,1,0:T(4,128)} %bitcast.6, f32[3,4,256]{2,1,0:T(4,128)} %bitcast.7, ...), custom_call_target="tpu_custom_call" | custom-call | tf_op jit(solution)/shard_map/pallas_call | solution.py:211
  1.5 0.1 collective-permute-start
  1.6 6.8 %collective-permute-start.1 = (f32[12,256]{1,0:T(8,128)S(1)}, f32[12,256]{1,0:T(8,128)S(1)}, u32[]{:S(2)}, u32[]{:S(2)}) collective-permute-start(f32[12,256]{1,0:T(8,128)S(1)} %get-tuple-element.33), channel_id=1, source_target_pairs={{4,8},{12,16},{20,24},{28,32},{36,40},{44,48},{52,56},{60,64},{68,... | collective-permute-start | bytes 36872 | tf_op jit(solution)/shard_map/ppermute | solution.py:224
  8.4 2.4 %shard_map.96 = (bf16[288,512]{1,0:T(8,128)(2,1)S(1)}, bf16[288,512]{1,0:T(8,128)(2,1)S(1)}, bf16[512,256]{1,0:T(8,128)(2,1)S(1)}, bf16[512,256]{1,0:T(8,128)(2,...) custom-call(s32[1,512]{1,0:T(1,128)S(1)} %get-tuple-element.34.sfirs, ...), custom_call_target="tpu_custom_call" | custom-call | tf_op jit(solution)/shard_map/pallas_call | solution.py:211
  10.8 0.0 collective-permute-done.near_ref
  10.8 0.1 collective-permute-done.1.far_ref
  10.9 0.1 shard_map.97
  11.0 0.1 collective-permute-start.2
  11.1 7.7 %collective-permute-start.3 = (f32[16,128]{1,0:T(8,128)S(1)}, f32[16,128]{1,0:T(8,128)S(1)}, u32[]{:S(2)}, u32[]{:S(2)}) collective-permute-start(f32[16,128]{1,0:T(8,128)S(1)} %get-tuple-element.43), channel_id=1, source_target_pairs={{1,2},{2,1},{5,6},{6,5},{9,10},{10,9},{13,14},{14,13},{17,18},{18,... | collective-permute-start | bytes 24584 | tf_op jit(solution)/shard_map/ppermute | solution.py:224
  18.9 0.4 shard_map.98.main_ref
  19.3 0.0 collective-permute-done.2.one_ref
  19.3 1.2 %collective-permute-done.3.two_ref = f32[16,128]{1,0:T(8,128)S(1)} collective-permute-done((f32[16,128]{1,0:T(8,128)S(1)}, f32[16,128]{1,0:T(8,128)S(1)}, u32[]{:S(2)}, u32[]{:S(2)}) %collective-permute-start.3) | collective-permute-done | bytes 8224 | tf_op jit(solution)/shard_map/ppermute | solution.py:224
  20.5 4.7 %shard_map.99 = (f32[256,128]{1,0:T(8,128)S(1)}, f32[16,128]{1,0:T(8,128)S(1)}, f32[16,128]{1,0:T(8,128)S(1)}) custom-call(f32[512,128]{1,0:T(8,128)S(1)} %shard_map.98.main_ref, f32[16,128]{1,0:T(8,128)S(1)} %collective-permute-done.2.one_ref, f32[16,128]{1,0:T(8,128)S(1)} %collective-permute-done.3.two_ref, ...), custom_call_target="tpu_custom_call" | custom-call | tf_op jit(solution)/shard_map/pallas_call | solution.py:211
  25.2 0.1 collective-permute-start.4
  25.3 6.0 %collective-permute-start.5 = (f32[16,128]{1,0:T(8,128)S(1)}, f32[16,128]{1,0:T(8,128)S(1)}, u32[]{:S(2)}, u32[]{:S(2)}) collective-permute-start(f32[16,128]{1,0:T(8,128)S(1)} %get-tuple-element.52), channel_id=1, source_target_pairs={{1,2},{2,1},{5,6},{6,5},{9,10},{10,9},{13,14},{14,13},{17,18},{18,... | collective-permute-start | bytes 24584 | tf_op jit(solution)/shard_map/ppermute | solution.py:224
  31.3 0.0 collective-permute-done.4.one_ref
  31.4 1.6 %collective-permute-done.5.two_ref = f32[16,128]{1,0:T(8,128)S(1)} collective-permute-done((f32[16,128]{1,0:T(8,128)S(1)}, f32[16,128]{1,0:T(8,128)S(1)}, u32[]{:S(2)}, u32[]{:S(2)}) %collective-permute-start.5) | collective-permute-done | bytes 8224 | tf_op jit(solution)/shard_map/ppermute | solution.py:224
  33.0 0.1 shard_map.100
  33.1 0.1 collective-permute-start.6
  33.2 4.5 %collective-permute-start.7 = (f32[12,256]{1,0:T(8,128)S(1)}, f32[12,256]{1,0:T(8,128)S(1)}, u32[]{:S(2)}, u32[]{:S(2)}) collective-permute-start(f32[12,256]{1,0:T(8,128)S(1)} %get-tuple-element.55), channel_id=1, source_target_pairs={{4,8},{12,16},{20,24},{28,32},{36,40},{44,48},{52,56},{60,64},{68,... | collective-permute-start | bytes 36872 | tf_op jit(solution)/shard_map/ppermute | solution.py:224
  37.7 0.0 collective-permute-done.6.refs_1_
  37.7 4.7 %collective-permute-done.7.refs_2_ = f32[12,256]{1,0:T(8,128)S(1)} collective-permute-done((f32[12,256]{1,0:T(8,128)S(1)}, f32[12,256]{1,0:T(8,128)S(1)}, u32[]{:S(2)}, u32[]{:S(2)}) %collective-permute-start.7) | collective-permute-done | bytes 12320 | tf_op jit(solution)/shard_map/ppermute | solution.py:224
  42.4 0.6 %shard_map.101 = (f32[3,4,256]{2,1,0:T(4,128)}, f32[3,4,256]{2,1,0:T(4,128)}) custom-call(f32[48,256]{1,0:T(8,128)S(1)} %get-tuple-element.53.refs_0_, f32[12,256]{1,0:T(8,128)S(1)} %collective-permute-done.6.refs_1_, f32[12,256]{1,0:T(8,128)S(1)} %collective-permute-done.7.refs_2_), custom_call_target="tpu_custom_call" | custom-call | tf_op jit(solution)/shard_map/pallas_call | solution.py:211
Async XLA Ops:
  1.5 9.3 %collective-permute-start = (f32[12,256]{1,0:T(8,128)S(1)}, f32[12,256]{1,0:T(8,128)S(1)}, u32[]{:S(2)}, u32[]{:S(2)}) collective-permute-start(f32[12,256]{1,0:T(8,128)S(1)} %get-tuple-element.32), channel_id=1, source_target_pairs={{0,4},{8,12},{16,20},{24,28},{32,36},{40,44},{48,52},{56,60},{64,6... | collective-permute-start | bytes 36872 | tf_op jit(solution)/shard_map/ppermute | solution.py:224
  1.6 9.3 %collective-permute-start.1 = (f32[12,256]{1,0:T(8,128)S(1)}, f32[12,256]{1,0:T(8,128)S(1)}, u32[]{:S(2)}, u32[]{:S(2)}) collective-permute-start(f32[12,256]{1,0:T(8,128)S(1)} %get-tuple-element.33), channel_id=1, source_target_pairs={{4,8},{12,16},{20,24},{28,32},{36,40},{44,48},{52,56},{60,64},{68,... | collective-permute-start | bytes 36872 | tf_op jit(solution)/shard_map/ppermute | solution.py:224
  11.0 8.2 %collective-permute-start.2 = (f32[16,128]{1,0:T(8,128)S(1)}, f32[16,128]{1,0:T(8,128)S(1)}, u32[]{:S(2)}, u32[]{:S(2)}) collective-permute-start(f32[16,128]{1,0:T(8,128)S(1)} %get-tuple-element.42), channel_id=1, source_target_pairs={{0,1},{2,3},{1,0},{3,2},{4,5},{6,7},{5,4},{7,6},{8,9},{10,11},{9,8... | collective-permute-start | bytes 24584 | tf_op jit(solution)/shard_map/ppermute | solution.py:224
  11.1 9.4 %collective-permute-start.3 = (f32[16,128]{1,0:T(8,128)S(1)}, f32[16,128]{1,0:T(8,128)S(1)}, u32[]{:S(2)}, u32[]{:S(2)}) collective-permute-start(f32[16,128]{1,0:T(8,128)S(1)} %get-tuple-element.43), channel_id=1, source_target_pairs={{1,2},{2,1},{5,6},{6,5},{9,10},{10,9},{13,14},{14,13},{17,18},{18,... | collective-permute-start | bytes 24584 | tf_op jit(solution)/shard_map/ppermute | solution.py:224
  25.2 6.1 %collective-permute-start.4 = (f32[16,128]{1,0:T(8,128)S(1)}, f32[16,128]{1,0:T(8,128)S(1)}, u32[]{:S(2)}, u32[]{:S(2)}) collective-permute-start(f32[16,128]{1,0:T(8,128)S(1)} %get-tuple-element.51), channel_id=1, source_target_pairs={{0,1},{2,3},{1,0},{3,2},{4,5},{6,7},{5,4},{7,6},{8,9},{10,11},{9,8... | collective-permute-start | bytes 24584 | tf_op jit(solution)/shard_map/ppermute | solution.py:224
  25.3 7.7 %collective-permute-start.5 = (f32[16,128]{1,0:T(8,128)S(1)}, f32[16,128]{1,0:T(8,128)S(1)}, u32[]{:S(2)}, u32[]{:S(2)}) collective-permute-start(f32[16,128]{1,0:T(8,128)S(1)} %get-tuple-element.52), channel_id=1, source_target_pairs={{1,2},{2,1},{5,6},{6,5},{9,10},{10,9},{13,14},{14,13},{17,18},{18,... | collective-permute-start | bytes 24584 | tf_op jit(solution)/shard_map/ppermute | solution.py:224
  33.1 4.7 %collective-permute-start.6 = (f32[12,256]{1,0:T(8,128)S(1)}, f32[12,256]{1,0:T(8,128)S(1)}, u32[]{:S(2)}, u32[]{:S(2)}) collective-permute-start(f32[12,256]{1,0:T(8,128)S(1)} %get-tuple-element.54), channel_id=1, source_target_pairs={{0,4},{8,12},{16,20},{24,28},{32,36},{40,44},{48,52},{56,60},{64,6... | collective-permute-start | bytes 36872 | tf_op jit(solution)/shard_map/ppermute | solution.py:224
  33.2 9.3 %collective-permute-start.7 = (f32[12,256]{1,0:T(8,128)S(1)}, f32[12,256]{1,0:T(8,128)S(1)}, u32[]{:S(2)}, u32[]{:S(2)}) collective-permute-start(f32[12,256]{1,0:T(8,128)S(1)} %get-tuple-element.55), channel_id=1, source_target_pairs={{4,8},{12,16},{20,24},{28,32},{36,40},{44,48},{52,56},{60,64},{68,... | collective-permute-start | bytes 36872 | tf_op jit(solution)/shard_map/ppermute | solution.py:224

commit v3 on v2

--- a/solution.py
+++ b/solution.py
@@ -4,6 +4,7 @@
 from jax.experimental import pallas as pl
 from jax.experimental.pallas import tpu as pltpu
 from jax.sharding import PartitionSpec as P
+
 
 HS = 16
 HT = 2
@@ -231,14 +232,14 @@
     periods, regions = lax.axis_size("tm"), lax.axis_size("cell")
 
     def over_tm(near, far):
-        return (
-            swap(near, "tm", [(t, t + 1) for t in range(0, periods, 2)]),
-            swap(far, "tm", [(t, t + 1) for t in range(1, periods - 1, 2)]),
-        )
+        far = swap(far, "tm", [(t, (t + 1) % periods) for t in range(1, periods, 2)])
+        near = swap(near, "tm", [(t, t + 1) for t in range(0, periods, 2)])
+        return near, far
 
     def over_cell(one, two):
-        second = swap(two, "cell", [(c, c + 1) for c in range(1, regions - 1, 2)])
-        return swap(one, "cell", [(c, c + 1) for c in range(0, regions, 2)]), second
+        two = swap(two, "cell", [(c, (c + 1) % regions) for c in range(1, regions, 2)])
+        one = swap(one, "cell", [(c, c + 1) for c in range(0, regions, 2)])
+        return one, two
 
     small = (jnp.swapaxes(theta, 1, 2), jnp.swapaxes(tangent, 1, 2), sfirst[None], sweight, tfirst[None], tweight)
     strip = ((12, rows), F32)

time: 43.9 us -> 39 us (0.89)
  the two profiles are of different devices: /device:TPU:96 before, /device:TPU:32 now
where the time goes in v3:
time: 39 us; the launch traced here: 38.8 us
  starting transfers between devices  20.8 us (53%)
  Pallas kernels  9.17 us (24%)
  waiting for transfers between devices  8.08 us (21%)
  between operations  0.71 us (2%)
    ppermute x8, starting transfers between devices, swap(): lax.ppermute(value, axis, [(a, b) for a, b in pairs] + [(b, a) for a, b i...  20.8 us
    pallas_call x7, Pallas kernels, run(): pl.pallas_call(kernel, out_shape=tuple((shape(s, d) for s, d in outs)), i...  9.17 us
    ppermute x8, waiting for transfers between devices, swap(): lax.ppermute(value, axis, [(a, b) for a, b in pairs] + [(b, a) for a, b i...  8.08 us
  transfers between devices with their start and end apart: 8, of which 4 were waited for; matrix products, arithmetic and copies ran while one was open for 0% of the time, Pallas kernels for 7%

profile of v3, /device:TPU:32, one launch (start us, length us, event | category | flops | bytes accessed | tf_op | source)
XLA Modules:
  0.0 38.8 jit_solution(9079846324578420439)
XLA Ops:
  0.6 0.9 %shard_map.95 = (f32[3,4,256]{2,1,0:T(4,128)S(1)}, f32[3,4,256]{2,1,0:T(4,128)S(1)}, s32[1,512]{1,0:T(1,128)S(1)}, f32[16,512]{1,0:T(8,128)S(1)}, s32[1,512]{1,0...) custom-call(f32[3,4,256]{2,1,0:T(4,128)} %bitcast.6, f32[3,4,256]{2,1,0:T(4,128)} %bitcast.7, ...), custom_call_target="tpu_custom_call" | custom-call | tf_op jit(solution)/shard_map/pallas_call | solution.py:212
  1.5 0.1 collective-permute-start
  1.6 4.9 %collective-permute-start.1 = (f32[12,256]{1,0:T(8,128)S(1)}, f32[12,256]{1,0:T(8,128)S(1)}, u32[]{:S(2)}, u32[]{:S(2)}) collective-permute-start(f32[12,256]{1,0:T(8,128)S(1)} %get-tuple-element.33), channel_id=1, source_target_pairs={{4,8},{12,16},{20,24},{28,32},{36,40},{44,48},{52,56},{60,64},{68,... | collective-permute-start | bytes 36872 | tf_op jit(solution)/shard_map/ppermute | solution.py:225
  6.5 2.4 %shard_map.96 = (bf16[288,512]{1,0:T(8,128)(2,1)S(1)}, bf16[288,512]{1,0:T(8,128)(2,1)S(1)}, bf16[512,256]{1,0:T(8,128)(2,1)S(1)}, bf16[512,256]{1,0:T(8,128)(2,...) custom-call(s32[1,512]{1,0:T(1,128)S(1)} %get-tuple-element.34.sfirs, ...), custom_call_target="tpu_custom_call" | custom-call | tf_op jit(solution)/shard_map/pallas_call | solution.py:212
  8.9 0.0 collective-permute-done.near_ref
  8.9 0.2 collective-permute-done.1.far_ref
  9.1 0.1 shard_map.97
  9.2 3.4 %collective-permute-start.2 = (f32[16,128]{1,0:T(8,128)S(1)}, f32[16,128]{1,0:T(8,128)S(1)}, u32[]{:S(2)}, u32[]{:S(2)}) collective-permute-start(f32[16,128]{1,0:T(8,128)S(1)} %get-tuple-element.42), channel_id=1, source_target_pairs={{0,1},{2,3},{1,0},{3,2},{4,5},{6,7},{5,4},{7,6},{8,9},{10,11},{9,8... | collective-permute-start | bytes 24584 | tf_op jit(solution)/shard_map/ppermute | solution.py:225
  12.6 4.3 %collective-permute-start.3 = (f32[16,128]{1,0:T(8,128)S(1)}, f32[16,128]{1,0:T(8,128)S(1)}, u32[]{:S(2)}, u32[]{:S(2)}) collective-permute-start(f32[16,128]{1,0:T(8,128)S(1)} %get-tuple-element.43), channel_id=1, source_target_pairs={{1,2},{3,0},{2,1},{0,3},{5,6},{7,4},{6,5},{4,7},{9,10},{11,8},{10,... | collective-permute-start | bytes 24584 | tf_op jit(solution)/shard_map/ppermute | solution.py:225
  16.9 0.4 shard_map.98.main_ref
  17.2 0.0 collective-permute-done.2.one_ref
  17.2 1.2 %collective-permute-done.3.two_ref = f32[16,128]{1,0:T(8,128)S(1)} collective-permute-done((f32[16,128]{1,0:T(8,128)S(1)}, f32[16,128]{1,0:T(8,128)S(1)}, u32[]{:S(2)}, u32[]{:S(2)}) %collective-permute-start.3) | collective-permute-done | bytes 8224 | tf_op jit(solution)/shard_map/ppermute | solution.py:225
  18.5 4.7 %shard_map.99 = (f32[256,128]{1,0:T(8,128)S(1)}, f32[16,128]{1,0:T(8,128)S(1)}, f32[16,128]{1,0:T(8,128)S(1)}) custom-call(f32[512,128]{1,0:T(8,128)S(1)} %shard_map.98.main_ref, f32[16,128]{1,0:T(8,128)S(1)} %collective-permute-done.2.one_ref, f32[16,128]{1,0:T(8,128)S(1)} %collective-permute-done.3.two_ref, ...), custom_call_target="tpu_custom_call" | custom-call | tf_op jit(solution)/shard_map/pallas_call | solution.py:212
  23.2 1.6 %collective-permute-start.4 = (f32[16,128]{1,0:T(8,128)S(1)}, f32[16,128]{1,0:T(8,128)S(1)}, u32[]{:S(2)}, u32[]{:S(2)}) collective-permute-start(f32[16,128]{1,0:T(8,128)S(1)} %get-tuple-element.51), channel_id=1, source_target_pairs={{0,1},{2,3},{1,0},{3,2},{4,5},{6,7},{5,4},{7,6},{8,9},{10,11},{9,8... | collective-permute-start | bytes 24584 | tf_op jit(solution)/shard_map/ppermute | solution.py:225
  24.8 4.1 %collective-permute-start.5 = (f32[16,128]{1,0:T(8,128)S(1)}, f32[16,128]{1,0:T(8,128)S(1)}, u32[]{:S(2)}, u32[]{:S(2)}) collective-permute-start(f32[16,128]{1,0:T(8,128)S(1)} %get-tuple-element.52), channel_id=1, source_target_pairs={{1,2},{3,0},{2,1},{0,3},{5,6},{7,4},{6,5},{4,7},{9,10},{11,8},{10,... | collective-permute-start | bytes 24584 | tf_op jit(solution)/shard_map/ppermute | solution.py:225
  28.9 0.0 collective-permute-done.4.one_ref
  28.9 1.6 %collective-permute-done.5.two_ref = f32[16,128]{1,0:T(8,128)S(1)} collective-permute-done((f32[16,128]{1,0:T(8,128)S(1)}, f32[16,128]{1,0:T(8,128)S(1)}, u32[]{:S(2)}, u32[]{:S(2)}) %collective-permute-start.5) | collective-permute-done | bytes 8224 | tf_op jit(solution)/shard_map/ppermute | solution.py:225
  30.5 0.1 shard_map.100
  30.6 0.1 collective-permute-start.6
  30.7 2.5 %collective-permute-start.7 = (f32[12,256]{1,0:T(8,128)S(1)}, f32[12,256]{1,0:T(8,128)S(1)}, u32[]{:S(2)}, u32[]{:S(2)}) collective-permute-start(f32[12,256]{1,0:T(8,128)S(1)} %get-tuple-element.55), channel_id=1, source_target_pairs={{4,8},{12,16},{20,24},{28,32},{36,40},{44,48},{52,56},{60,64},{68,... | collective-permute-start | bytes 36872 | tf_op jit(solution)/shard_map/ppermute | solution.py:225
  33.2 0.0 collective-permute-done.6.refs_1_
  33.2 5.0 %collective-permute-done.7.refs_2_ = f32[12,256]{1,0:T(8,128)S(1)} collective-permute-done((f32[12,256]{1,0:T(8,128)S(1)}, f32[12,256]{1,0:T(8,128)S(1)}, u32[]{:S(2)}, u32[]{:S(2)}) %collective-permute-start.7) | collective-permute-done | bytes 12320 | tf_op jit(solution)/shard_map/ppermute | solution.py:225
  38.2 0.6 %shard_map.101 = (f32[3,4,256]{2,1,0:T(4,128)}, f32[3,4,256]{2,1,0:T(4,128)}) custom-call(f32[48,256]{1,0:T(8,128)S(1)} %get-tuple-element.53.refs_0_, f32[12,256]{1,0:T(8,128)S(1)} %collective-permute-done.6.refs_1_, f32[12,256]{1,0:T(8,128)S(1)} %collective-permute-done.7.refs_2_), custom_call_target="tpu_custom_call" | custom-call | tf_op jit(solution)/shard_map/pallas_call | solution.py:212
Async XLA Ops:
  1.5 7.4 %collective-permute-start = (f32[12,256]{1,0:T(8,128)S(1)}, f32[12,256]{1,0:T(8,128)S(1)}, u32[]{:S(2)}, u32[]{:S(2)}) collective-permute-start(f32[12,256]{1,0:T(8,128)S(1)} %get-tuple-element.32), channel_id=1, source_target_pairs={{0,4},{8,12},{16,20},{24,28},{32,36},{40,44},{48,52},{56,60},{64,6... | collective-permute-start | bytes 36872 | tf_op jit(solution)/shard_map/ppermute | solution.py:225
  1.6 7.5 %collective-permute-start.1 = (f32[12,256]{1,0:T(8,128)S(1)}, f32[12,256]{1,0:T(8,128)S(1)}, u32[]{:S(2)}, u32[]{:S(2)}) collective-permute-start(f32[12,256]{1,0:T(8,128)S(1)} %get-tuple-element.33), channel_id=1, source_target_pairs={{4,8},{12,16},{20,24},{28,32},{36,40},{44,48},{52,56},{60,64},{68,... | collective-permute-start | bytes 36872 | tf_op jit(solution)/shard_map/ppermute | solution.py:225
  9.2 8.0 %collective-permute-start.2 = (f32[16,128]{1,0:T(8,128)S(1)}, f32[16,128]{1,0:T(8,128)S(1)}, u32[]{:S(2)}, u32[]{:S(2)}) collective-permute-start(f32[16,128]{1,0:T(8,128)S(1)} %get-tuple-element.42), channel_id=1, source_target_pairs={{0,1},{2,3},{1,0},{3,2},{4,5},{6,7},{5,4},{7,6},{8,9},{10,11},{9,8... | collective-permute-start | bytes 24584 | tf_op jit(solution)/shard_map/ppermute | solution.py:225
  12.6 5.9 %collective-permute-start.3 = (f32[16,128]{1,0:T(8,128)S(1)}, f32[16,128]{1,0:T(8,128)S(1)}, u32[]{:S(2)}, u32[]{:S(2)}) collective-permute-start(f32[16,128]{1,0:T(8,128)S(1)} %get-tuple-element.43), channel_id=1, source_target_pairs={{1,2},{3,0},{2,1},{0,3},{5,6},{7,4},{6,5},{4,7},{9,10},{11,8},{10,... | collective-permute-start | bytes 24584 | tf_op jit(solution)/shard_map/ppermute | solution.py:225
  23.2 5.7 %collective-permute-start.4 = (f32[16,128]{1,0:T(8,128)S(1)}, f32[16,128]{1,0:T(8,128)S(1)}, u32[]{:S(2)}, u32[]{:S(2)}) collective-permute-start(f32[16,128]{1,0:T(8,128)S(1)} %get-tuple-element.51), channel_id=1, source_target_pairs={{0,1},{2,3},{1,0},{3,2},{4,5},{6,7},{5,4},{7,6},{8,9},{10,11},{9,8... | collective-permute-start | bytes 24584 | tf_op jit(solution)/shard_map/ppermute | solution.py:225
  24.8 5.8 %collective-permute-start.5 = (f32[16,128]{1,0:T(8,128)S(1)}, f32[16,128]{1,0:T(8,128)S(1)}, u32[]{:S(2)}, u32[]{:S(2)}) collective-permute-start(f32[16,128]{1,0:T(8,128)S(1)} %get-tuple-element.52), channel_id=1, source_target_pairs={{1,2},{3,0},{2,1},{0,3},{5,6},{7,4},{6,5},{4,7},{9,10},{11,8},{10,... | collective-permute-start | bytes 24584 | tf_op jit(solution)/shard_map/ppermute | solution.py:225
  30.6 2.6 %collective-permute-start.6 = (f32[12,256]{1,0:T(8,128)S(1)}, f32[12,256]{1,0:T(8,128)S(1)}, u32[]{:S(2)}, u32[]{:S(2)}) collective-permute-start(f32[12,256]{1,0:T(8,128)S(1)} %get-tuple-element.54), channel_id=1, source_target_pairs={{0,4},{8,12},{16,20},{24,28},{32,36},{40,44},{48,52},{56,60},{64,6... | collective-permute-start | bytes 36872 | tf_op jit(solution)/shard_map/ppermute | solution.py:225
  30.7 7.5 %collective-permute-start.7 = (f32[12,256]{1,0:T(8,128)S(1)}, f32[12,256]{1,0:T(8,128)S(1)}, u32[]{:S(2)}, u32[]{:S(2)}) collective-permute-start(f32[12,256]{1,0:T(8,128)S(1)} %get-tuple-element.55), channel_id=1, source_target_pairs={{4,8},{12,16},{20,24},{28,32},{36,40},{44,48},{52,56},{60,64},{68,... | collective-permute-start | bytes 36872 | tf_op jit(solution)/shard_map/ppermute | solution.py:225

commit v4 on v3

--- a/solution.py
+++ b/solution.py
@@ -124,7 +124,7 @@
 
 def main_kernel(
     main_ref, one_ref, two_ref, edge_ref, spread_ref, gather_ref, shigh_ref, slow_ref, cov_ref, counts_ref,
-    own_ref, send_one_ref, send_two_ref, fields, whigh, wlow,
+    own_ref, send_one_ref, send_two_ref, fields, weighted, sums,
 ):
     odd = parity("cell") == 1
     one, two = one_ref[...], two_ref[...]
@@ -138,13 +138,16 @@
         [jnp.where(left, high, spatial - high).astype(BF16), jnp.where(left, high, 0.0).astype(BF16)[:, :64]], axis=1
     )
 
+    cells = fields.shape[1]
+
     def forward(j):
         fields[j] = dot(factor, spread_ref[j])
 
     def weigh(j):
         lanes = slice(128 * j, 128 * j + 128)
-        for start in range(0, fields.shape[1], 16):
+        for start in range(0, cells, 16):
             rows = slice(start, start + 16)
+            lower_rows = slice(cells + start, cells + start + 16)
             cov = [cov_ref[k, rows, lanes] for k in range(3)]
             at = [fields[j, rows, 128 * pk : 128 * pk + 128] for pk in range(6)]
             rates = jnp.exp(cov[0] * at[0] + cov[1] * at[1] + cov[2] * at[2])
@@ -153,12 +156,11 @@
             for p, value in enumerate((slope, excess)):
                 for k in range(3):
                     columns = slice(128 * (3 * p + k), 128 * (3 * p + k) + 128)
-                    upper, lower = split(cov[k] * value)
-                    whigh[j, rows, columns] = upper
-                    wlow[j, rows, columns] = lower
+                    weighted[j, rows, columns], weighted[j, lower_rows, columns] = split(cov[k] * value)
 
     def back(j):
-        return dot(whigh[j], gather_ref[j]) + dot(wlow[j], gather_ref[j])
+        both = dot(weighted[j], gather_ref[j])
+        return both[:cells] + both[cells:]
 
     forward(0)
     total = jnp.zeros(spatial.shape, F32)
@@ -169,9 +171,10 @@
         if j > 0:
             total = total + back(j - 1)
     total = total + back(3)
-    total = total + pltpu.roll(total, 64, 1)
     total_high, total_low = split(total)
-    summed = dot(shigh_ref[...], total_high) + dot(slow_ref[...], total_high) + dot(shigh_ref[...], total_low)
+    whole = dot(shigh_ref[...], jnp.concatenate([total_high, total_low], axis=1))
+    summed = whole[:, :128] + whole[:, 128:] + dot(slow_ref[...], total_high)
+    summed = summed + pltpu.roll(summed, 64, 1)
     count = own_ref.shape[0]
     own_ref[...] = summed[HS : HS + count]
     low, high = summed[:HS], summed[HS + count :]
@@ -221,24 +224,35 @@
     return run
 
 
-def swap(value, axis, pairs):
-    return lax.ppermute(value, axis, [(a, b) for a, b in pairs] + [(b, a) for a, b in pairs])
-
-
 def body(theta, tangent, covariates, counts, sfirst, sweight, tfirst, tweight):
     hours = counts.shape[1]
     rows = theta.shape[1]
     cells = counts.shape[0]
     periods, regions = lax.axis_size("tm"), lax.axis_size("cell")
 
+    every = [(t, c) for t in range(periods) for c in range(regions)]
+
+    def swap(value, partner):
+        return lax.ppermute(value, ("tm", "cell"), [(t * regions + c, partner(t, c)) for t, c in every])
+
+    def far_of(t, c):
+        if t in (0, periods - 1):
+            return t * regions + (c ^ 1)
+        return (t + 1 if t % 2 else t - 1) * regions + c
+
+    def two_of(t, c):
+        if c in (0, regions - 1):
+            return (t ^ 1) * regions + c
+        return t * regions + (c + 1 if c % 2 else c - 1)
+
     def over_tm(near, far):
-        far = swap(far, "tm", [(t, (t + 1) % periods) for t in range(1, periods, 2)])
-        near = swap(near, "tm", [(t, t + 1) for t in range(0, periods, 2)])
+        far = swap(far, far_of)
+        near = swap(near, lambda t, c: (t ^ 1) * regions + c)
         return near, far
 
     def over_cell(one, two):
-        two = swap(two, "cell", [(c, (c + 1) % regions) for c in range(1, regions, 2)])
-        one = swap(one, "cell", [(c, c + 1) for c in range(0, regions, 2)])
+        two = swap(two, two_of)
+        one = swap(one, lambda t, c: t * regions + (c ^ 1))
         return one, two
 
     small = (jnp.swapaxes(theta, 1, 2), jnp.swapaxes(tangent, 1, 2), sfirst[None], sweight, tfirst[None], tweight)
@@ -266,7 +280,7 @@
     own, one, two = call(
         main_kernel,
         [((rows, 128), F32), band, band],
-        [pltpu.VMEM((4, cells, 768), F32), pltpu.VMEM((4, cells, 768), BF16), pltpu.VMEM((4, cells, 768), BF16)],
+        [pltpu.VMEM((4, cells, 768), F32), pltpu.VMEM((4, 2 * cells, 768), BF16), pltpu.VMEM((cells, 128), F32)],
     )(main, one, two, edge, spread, gather, shigh, slow, covariates, counts)
     one, two = over_cell(one, two)
     wide, near, far = call(turn_kernel, [((48, rows), F32), strip, strip])(own, one, two)

time: 39 us -> 35.9 us (0.921)
  the two profiles are of different devices: /device:TPU:32 before, /device:TPU:160 now
where the time goes in v4:
time: 35.9 us; the launch traced here: 35.7 us
  waiting for transfers between devices  16.1 us (45%)
  starting transfers between devices  10.2 us (28%)
  Pallas kernels  8.72 us (24%)
  between operations  0.72 us (2%)
    ppermute x8, waiting for transfers between devices, swap(): lax.ppermute(value, ('tm', 'cell'), [(t * regions + c, partner(t, c)) for...  16.1 us
    ppermute x8, starting transfers between devices, swap(): lax.ppermute(value, ('tm', 'cell'), [(t * regions + c, partner(t, c)) for...  10.2 us
    pallas_call x7, Pallas kernels, run(): pl.pallas_call(kernel, out_shape=tuple((shape(s, d) for s, d in outs)), i...  8.72 us
  transfers between devices with their start and end apart: 8, of which 5 were waited for; matrix products, arithmetic and copies ran while one was open for 0% of the time, Pallas kernels for 8%

profile of v4, /device:TPU:160, one launch (start us, length us, event | category | flops | bytes accessed | tf_op | source)
XLA Modules:
  0.0 35.7 jit_solution(6948715055846034276)
XLA Ops:
  0.6 0.9 %shard_map.95 = (f32[3,4,256]{2,1,0:T(4,128)S(1)}, f32[3,4,256]{2,1,0:T(4,128)S(1)}, s32[1,512]{1,0:T(1,128)S(1)}, f32[16,512]{1,0:T(8,128)S(1)}, s32[1,512]{1,0...) custom-call(f32[3,4,256]{2,1,0:T(4,128)} %bitcast.6, f32[3,4,256]{2,1,0:T(4,128)} %bitcast.7, ...), custom_call_target="tpu_custom_call" | custom-call | tf_op jit(solution)/shard_map/pallas_call | solution.py:215
  1.5 0.1 collective-permute-start
  1.6 5.8 %collective-permute-start.1 = (f32[12,256]{1,0:T(8,128)S(1)}, f32[12,256]{1,0:T(8,128)S(1)}, u32[]{:S(2)}, u32[]{:S(2)}) collective-permute-start(f32[12,256]{1,0:T(8,128)S(1)} %get-tuple-element.33), channel_id=1, source_target_pairs={{0,1},{1,0},{2,3},{3,2},{4,8},{5,9},{6,10},{7,11},{8,4},{9,5},{10,... | collective-permute-start | bytes 36872 | tf_op jit(solution)/shard_map/ppermute | solution.py:236
  7.4 2.4 %shard_map.96 = (bf16[288,512]{1,0:T(8,128)(2,1)S(1)}, bf16[288,512]{1,0:T(8,128)(2,1)S(1)}, bf16[512,256]{1,0:T(8,128)(2,1)S(1)}, bf16[512,256]{1,0:T(8,128)(2,...) custom-call(s32[1,512]{1,0:T(1,128)S(1)} %get-tuple-element.34.sfirs, ...), custom_call_target="tpu_custom_call" | custom-call | tf_op jit(solution)/shard_map/pallas_call | solution.py:215
  9.8 0.0 collective-permute-done.near_ref
  9.8 0.0 collective-permute-done.1.far_ref
  9.8 0.1 shard_map.97
  9.9 1.6 %collective-permute-start.2 = (f32[16,128]{1,0:T(8,128)S(1)}, f32[16,128]{1,0:T(8,128)S(1)}, u32[]{:S(2)}, u32[]{:S(2)}) collective-permute-start(f32[16,128]{1,0:T(8,128)S(1)} %get-tuple-element.42), channel_id=1, source_target_pairs={{0,1},{1,0},{2,3},{3,2},{4,5},{5,4},{6,7},{7,6},{8,9},{9,8},{10,11... | collective-permute-start | bytes 24584 | tf_op jit(solution)/shard_map/ppermute | solution.py:236
  11.5 0.0 collective-permute-start.3
  11.5 0.4 %shard_map.98.main_ref = f32[512,128]{1,0:T(8,128)S(1)} custom-call(f32[256,128]{1,0:T(8,128)S(1)} %get-tuple-element.39.coef_ref, bf16[512,256]{1,0:T(8,128)(2,1)S(1)} %get-tuple-element.40.high_ref, bf16[512,256]{1,0:T(8,128)(2,1)S(1)} %get-tuple-element.41.low_ref), custom_call_target="tpu_custom_call" | custom-call | tf_op jit(solution)/shard_map/pallas_call | solution.py:215
  11.9 2.7 %collective-permute-done.2.one_ref = f32[16,128]{1,0:T(8,128)S(1)} collective-permute-done((f32[16,128]{1,0:T(8,128)S(1)}, f32[16,128]{1,0:T(8,128)S(1)}, u32[]{:S(2)}, u32[]{:S(2)}) %collective-permute-start.2) | collective-permute-done | bytes 8224 | tf_op jit(solution)/shard_map/ppermute | solution.py:236
  14.6 2.7 %collective-permute-done.3.two_ref = f32[16,128]{1,0:T(8,128)S(1)} collective-permute-done((f32[16,128]{1,0:T(8,128)S(1)}, f32[16,128]{1,0:T(8,128)S(1)}, u32[]{:S(2)}, u32[]{:S(2)}) %collective-permute-start.3) | collective-permute-done | bytes 8224 | tf_op jit(solution)/shard_map/ppermute | solution.py:236
  17.2 4.2 %shard_map.99 = (f32[256,128]{1,0:T(8,128)S(1)}, f32[16,128]{1,0:T(8,128)S(1)}, f32[16,128]{1,0:T(8,128)S(1)}) custom-call(f32[512,128]{1,0:T(8,128)S(1)} %shard_map.98.main_ref, f32[16,128]{1,0:T(8,128)S(1)} %collective-permute-done.2.one_ref, f32[16,128]{1,0:T(8,128)S(1)} %collective-permute-done.3.two_ref, ...), custom_call_target="tpu_custom_call" | custom-call | tf_op jit(solution)/shard_map/pallas_call | solution.py:215
  21.5 0.1 collective-permute-start.4
  21.6 0.1 collective-permute-start.5
  21.7 4.4 %collective-permute-done.4.one_ref = f32[16,128]{1,0:T(8,128)S(1)} collective-permute-done((f32[16,128]{1,0:T(8,128)S(1)}, f32[16,128]{1,0:T(8,128)S(1)}, u32[]{:S(2)}, u32[]{:S(2)}) %collective-permute-start.4) | collective-permute-done | bytes 8224 | tf_op jit(solution)/shard_map/ppermute | solution.py:236
  26.1 1.3 %collective-permute-done.5.two_ref = f32[16,128]{1,0:T(8,128)S(1)} collective-permute-done((f32[16,128]{1,0:T(8,128)S(1)}, f32[16,128]{1,0:T(8,128)S(1)}, u32[]{:S(2)}, u32[]{:S(2)}) %collective-permute-start.5) | collective-permute-done | bytes 8224 | tf_op jit(solution)/shard_map/ppermute | solution.py:236
  27.4 0.1 shard_map.100
  27.5 0.1 collective-permute-start.6
  27.6 2.5 %collective-permute-start.7 = (f32[12,256]{1,0:T(8,128)S(1)}, f32[12,256]{1,0:T(8,128)S(1)}, u32[]{:S(2)}, u32[]{:S(2)}) collective-permute-start(f32[12,256]{1,0:T(8,128)S(1)} %get-tuple-element.55), channel_id=1, source_target_pairs={{0,1},{1,0},{2,3},{3,2},{4,8},{5,9},{6,10},{7,11},{8,4},{9,5},{10,... | collective-permute-start | bytes 36872 | tf_op jit(solution)/shard_map/ppermute | solution.py:236
  30.1 0.0 collective-permute-done.6.refs_1_
  30.1 5.0 %collective-permute-done.7.refs_2_ = f32[12,256]{1,0:T(8,128)S(1)} collective-permute-done((f32[12,256]{1,0:T(8,128)S(1)}, f32[12,256]{1,0:T(8,128)S(1)}, u32[]{:S(2)}, u32[]{:S(2)}) %collective-permute-start.7) | collective-permute-done | bytes 12320 | tf_op jit(solution)/shard_map/ppermute | solution.py:236
  35.1 0.6 %shard_map.101 = (f32[3,4,256]{2,1,0:T(4,128)}, f32[3,4,256]{2,1,0:T(4,128)}) custom-call(f32[48,256]{1,0:T(8,128)S(1)} %get-tuple-element.53.refs_0_, f32[12,256]{1,0:T(8,128)S(1)} %collective-permute-done.6.refs_1_, f32[12,256]{1,0:T(8,128)S(1)} %collective-permute-done.7.refs_2_), custom_call_target="tpu_custom_call" | custom-call | tf_op jit(solution)/shard_map/pallas_call | solution.py:215
Async XLA Ops:
  1.5 8.3 %collective-permute-start = (f32[12,256]{1,0:T(8,128)S(1)}, f32[12,256]{1,0:T(8,128)S(1)}, u32[]{:S(2)}, u32[]{:S(2)}) collective-permute-start(f32[12,256]{1,0:T(8,128)S(1)} %get-tuple-element.32), channel_id=1, source_target_pairs={{0,4},{1,5},{2,6},{3,7},{4,0},{5,1},{6,2},{7,3},{8,12},{9,13},{10,... | collective-permute-start | bytes 36872 | tf_op jit(solution)/shard_map/ppermute | solution.py:236
  1.6 8.2 %collective-permute-start.1 = (f32[12,256]{1,0:T(8,128)S(1)}, f32[12,256]{1,0:T(8,128)S(1)}, u32[]{:S(2)}, u32[]{:S(2)}) collective-permute-start(f32[12,256]{1,0:T(8,128)S(1)} %get-tuple-element.33), channel_id=1, source_target_pairs={{0,1},{1,0},{2,3},{3,2},{4,8},{5,9},{6,10},{7,11},{8,4},{9,5},{10,... | collective-permute-start | bytes 36872 | tf_op jit(solution)/shard_map/ppermute | solution.py:236
  9.9 4.6 %collective-permute-start.2 = (f32[16,128]{1,0:T(8,128)S(1)}, f32[16,128]{1,0:T(8,128)S(1)}, u32[]{:S(2)}, u32[]{:S(2)}) collective-permute-start(f32[16,128]{1,0:T(8,128)S(1)} %get-tuple-element.42), channel_id=1, source_target_pairs={{0,1},{1,0},{2,3},{3,2},{4,5},{5,4},{6,7},{7,6},{8,9},{9,8},{10,11... | collective-permute-start | bytes 24584 | tf_op jit(solution)/shard_map/ppermute | solution.py:236
  11.5 5.8 %collective-permute-start.3 = (f32[16,128]{1,0:T(8,128)S(1)}, f32[16,128]{1,0:T(8,128)S(1)}, u32[]{:S(2)}, u32[]{:S(2)}) collective-permute-start(f32[16,128]{1,0:T(8,128)S(1)} %get-tuple-element.43), channel_id=1, source_target_pairs={{0,4},{1,2},{2,1},{3,7},{4,0},{5,6},{6,5},{7,3},{8,12},{9,10},{10,... | collective-permute-start | bytes 24584 | tf_op jit(solution)/shard_map/ppermute | solution.py:236
  21.5 4.6 %collective-permute-start.4 = (f32[16,128]{1,0:T(8,128)S(1)}, f32[16,128]{1,0:T(8,128)S(1)}, u32[]{:S(2)}, u32[]{:S(2)}) collective-permute-start(f32[16,128]{1,0:T(8,128)S(1)} %get-tuple-element.51), channel_id=1, source_target_pairs={{0,1},{1,0},{2,3},{3,2},{4,5},{5,4},{6,7},{7,6},{8,9},{9,8},{10,11... | collective-permute-start | bytes 24584 | tf_op jit(solution)/shard_map/ppermute | solution.py:236
  21.6 5.8 %collective-permute-start.5 = (f32[16,128]{1,0:T(8,128)S(1)}, f32[16,128]{1,0:T(8,128)S(1)}, u32[]{:S(2)}, u32[]{:S(2)}) collective-permute-start(f32[16,128]{1,0:T(8,128)S(1)} %get-tuple-element.52), channel_id=1, source_target_pairs={{0,4},{1,2},{2,1},{3,7},{4,0},{5,6},{6,5},{7,3},{8,12},{9,10},{10,... | collective-permute-start | bytes 24584 | tf_op jit(solution)/shard_map/ppermute | solution.py:236
  27.5 2.6 %collective-permute-start.6 = (f32[12,256]{1,0:T(8,128)S(1)}, f32[12,256]{1,0:T(8,128)S(1)}, u32[]{:S(2)}, u32[]{:S(2)}) collective-permute-start(f32[12,256]{1,0:T(8,128)S(1)} %get-tuple-element.54), channel_id=1, source_target_pairs={{0,4},{1,5},{2,6},{3,7},{4,0},{5,1},{6,2},{7,3},{8,12},{9,13},{10,... | collective-permute-start | bytes 36872 | tf_op jit(solution)/shard_map/ppermute | solution.py:236
  27.6 7.5 %collective-permute-start.7 = (f32[12,256]{1,0:T(8,128)S(1)}, f32[12,256]{1,0:T(8,128)S(1)}, u32[]{:S(2)}, u32[]{:S(2)}) collective-permute-start(f32[12,256]{1,0:T(8,128)S(1)} %get-tuple-element.55), channel_id=1, source_target_pairs={{0,1},{1,0},{2,3},{3,2},{4,8},{5,9},{6,10},{7,11},{8,4},{9,5},{10,... | collective-permute-start | bytes 36872 | tf_op jit(solution)/shard_map/ppermute | solution.py:236

commit v5 on v4

--- a/solution.py
+++ b/solution.py
@@ -24,6 +24,15 @@
 
 def dot(a, b):
     return jnp.dot(a, b, preferred_element_type=F32)
+
+
+def fold(x):
+    return jnp.where(iota((8, 128), 1) < 64, x[:8], x[8:])
+
+
+def unfold(x):
+    other, left = pltpu.roll(x, 64, 1), iota(x.shape, 1) < 64
+    return jnp.concatenate([jnp.where(left, x, other), jnp.where(left, other, x)], axis=0)
 
 
 def parity(axis):
@@ -59,15 +68,15 @@
                 wide[base + 8 * pk + 6 : base + 8 * pk + 8, :] = jnp.where(odd, far, near)
     turned = wide[...].T
     coef_ref[...] = turned
-    low, high = turned[0:HS], turned[turned.shape[0] - HS :]
+    low, high = fold(turned[0:HS]), fold(turned[turned.shape[0] - HS :])
     below = parity("cell") == 1
     one_ref[...] = jnp.where(below, low, high)
     two_ref[...] = jnp.where(below, high, low)
 
 
 def basis_kernel(
-    sfirst_ref, sweight_ref, tfirst_ref, tweight_ref, cov_any, counts_any,
-    shigh_ref, slow_ref, turned_high_ref, turned_low_ref, edge_ref, spread_ref, gather_ref, cov_ref, counts_ref, sems,
+    sfirst_ref, sweight_ref, cov_any, counts_any,
+    shigh_ref, slow_ref, turned_high_ref, turned_low_ref, edge_ref, cov_ref, counts_ref, sems,
 ):
     copies = (pltpu.make_async_copy(cov_any, cov_ref, sems.at[0]), pltpu.make_async_copy(counts_any, counts_ref, sems.at[1]))
     for copy in copies:
@@ -93,7 +102,13 @@
     edge_high, edge_low = split(edge_all)
     part = iota(edge_all.shape, 1) // 32
     edge_ref[...] = jnp.where(part == 1, edge_low.astype(F32), edge_high.astype(F32)).astype(BF16)
-
+    for copy in copies:
+        copy.wait()
+
+
+def inner_kernel(coef_ref, high_ref, low_ref, tfirst_ref, tweight_ref, main_ref, spread_ref, gather_ref):
+    coef_high, coef_low = split(coef_ref[...])
+    main_ref[...] = dot(high_ref[...], coef_high) + dot(low_ref[...], coef_high) + dot(high_ref[...], coef_low)
     tfirst = tfirst_ref[...] - (lax.axis_index("tm") * 4 - HT)
     hours = tfirst.shape[1]
     row = iota((192, hours), 0)
@@ -113,21 +128,15 @@
         for j in range(4):
             spread_ref[j, :, 128 * pk : 128 * pk + 128] = mine[:, 128 * j : 128 * j + 128]
             gather_ref[j, 128 * pk : 128 * pk + 128, :] = back[128 * j : 128 * j + 128, :]
-    for copy in copies:
-        copy.wait()
-
-
-def inner_kernel(coef_ref, high_ref, low_ref, main_ref):
-    coef_high, coef_low = split(coef_ref[...])
-    main_ref[...] = dot(high_ref[...], coef_high) + dot(low_ref[...], coef_high) + dot(high_ref[...], coef_low)
 
 
 def main_kernel(
-    main_ref, one_ref, two_ref, edge_ref, spread_ref, gather_ref, shigh_ref, slow_ref, cov_ref, counts_ref,
+    main_ref, first_ref, two_ref, third_ref, edge_ref, spread_ref, gather_ref, shigh_ref, slow_ref, cov_ref, counts_ref,
     own_ref, send_one_ref, send_two_ref, fields, weighted, sums,
 ):
     odd = parity("cell") == 1
-    one, two = one_ref[...], two_ref[...]
+    one = jnp.where(lax.axis_index("cell") < 2, first_ref[...], third_ref[...])
+    one, two = unfold(one), unfold(two_ref[...])
     halo = jnp.concatenate([jnp.where(odd, one, two), jnp.where(odd, two, one)], axis=0)
     halo_high, halo_low = split(halo)
     stacked = jnp.concatenate([halo_high, halo_high, halo_low, jnp.zeros_like(halo_low)], axis=0)
@@ -177,14 +186,14 @@
     summed = summed + pltpu.roll(summed, 64, 1)
     count = own_ref.shape[0]
     own_ref[...] = summed[HS : HS + count]
-    low, high = summed[:HS], summed[HS + count :]
+    low, high = fold(summed[:HS]), fold(summed[HS + count :])
     send_one_ref[...] = jnp.where(odd, low, high)
     send_two_ref[...] = jnp.where(odd, high, low)
 
 
 def turn_kernel(own_ref, one_ref, two_ref, wide_ref, near_ref, far_ref):
     below = parity("cell") == 1
-    one, two = one_ref[...], two_ref[...]
+    one, two = unfold(one_ref[...]), unfold(two_ref[...])
     count = own_ref.shape[0]
     low = own_ref[:HS] + jnp.where(below, one, two)
     high = own_ref[count - HS :] + jnp.where(below, two, one)
@@ -250,6 +259,15 @@
         near = swap(near, lambda t, c: (t ^ 1) * regions + c)
         return near, far
 
+    def side_of(first):
+        return lambda t, c: t * regions + (c ^ 1) if (c < regions // 2) == first else (t ^ 1) * regions + c
+
+    def over_cell_in_three(one, two):
+        low = swap(one, side_of(True))
+        two = swap(two, two_of)
+        high = swap(one, side_of(False))
+        return low, two, high
+
     def over_cell(one, two):
         two = swap(two, two_of)
         one = swap(one, lambda t, c: t * regions + (c ^ 1))
@@ -257,31 +275,33 @@
 
     small = (jnp.swapaxes(theta, 1, 2), jnp.swapaxes(tangent, 1, 2), sfirst[None], sweight, tfirst[None], tweight)
     strip = ((12, rows), F32)
-    band = ((HS, 128), F32)
+    band = ((HS // 2, 128), F32)
     theta_t, tangent_t, *support, near, far = call(
         load_kernel, [(a.shape, a.dtype) for a in small] + [strip, strip], [pltpu.SemaphoreType.DMA((6,))], apart=range(6)
     )(*small)
     near, far = over_tm(near, far)
     span = rows + 2 * HS
-    shigh, slow, turned_high, turned_low, edge, spread, gather, covariates, counts = call(
+    shigh, slow, turned_high, turned_low, edge, covariates, counts = call(
         basis_kernel,
         [
             ((span, cells), BF16), ((span, cells), BF16), ((cells, rows), BF16), ((cells, rows), BF16), ((cells, 128), BF16),
-            ((4, 192, 768), BF16), ((4, 768, 128), BF16), (covariates.shape, F32), (counts.shape, counts.dtype),
+            (covariates.shape, F32), (counts.shape, counts.dtype),
         ],
         [pltpu.SemaphoreType.DMA((2,))],
-        apart=(4, 5),
-    )(*support, covariates, counts)
+        apart=(2, 3),
+    )(*support[:2], covariates, counts)
     coef, one, two = call(widen_kernel, [((rows, 128), F32), band, band], [pltpu.VMEM((128, rows), F32)])(
         theta_t, tangent_t, near, far, edge
     )
-    one, two = over_cell(one, two)
-    (main,) = call(inner_kernel, [((cells, 128), F32)])(coef, turned_high, turned_low)
+    low, two, high = over_cell_in_three(one, two)
+    main, spread, gather = call(inner_kernel, [((cells, 128), F32), ((4, 192, 768), BF16), ((4, 768, 128), BF16)])(
+        coef, turned_high, turned_low, *support[2:]
+    )
     own, one, two = call(
         main_kernel,
         [((rows, 128), F32), band, band],
         [pltpu.VMEM((4, cells, 768), F32), pltpu.VMEM((4, 2 * cells, 768), BF16), pltpu.VMEM((cells, 128), F32)],
-    )(main, one, two, edge, spread, gather, shigh, slow, covariates, counts)
+    )(main, low, two, high, edge, spread, gather, shigh, slow, covariates, counts)
     one, two = over_cell(one, two)
     wide, near, far = call(turn_kernel, [((48, rows), F32), strip, strip])(own, one, two)
     near, far = over_tm(near, far)

time: 35.9 us -> 36.7 us (1.022)
  the two profiles are of different devices: /device:TPU:160 before, /device:TPU:95 now
where the time goes in v5:
time: 36.7 us; the launch traced here: 36.5 us
  starting transfers between devices  14.6 us (40%)
  waiting for transfers between devices  12.2 us (33%)
  Pallas kernels  9.03 us (25%)
  between operations  0.73 us (2%)
    ppermute x9, starting transfers between devices, swap(): lax.ppermute(value, ('tm', 'cell'), [(t * regions + c, partner(t, c)) for...  14.6 us
    ppermute x9, waiting for transfers between devices, swap(): lax.ppermute(value, ('tm', 'cell'), [(t * regions + c, partner(t, c)) for...  12.2 us
    pallas_call x7, Pallas kernels, run(): pl.pallas_call(kernel, out_shape=tuple((shape(s, d) for s, d in outs)), i...  9.03 us
  transfers between devices with their start and end apart: 9, of which 5 were waited for; matrix products, arithmetic and copies ran while one was open for 0% of the time, Pallas kernels for 8%

profile of v5, /device:TPU:95, one launch (start us, length us, event | category | flops | bytes accessed | tf_op | source)
XLA Modules:
  0.0 36.5 jit_solution(15067455491960676415)
XLA Ops:
  0.6 0.9 %shard_map.95 = (f32[3,4,256]{2,1,0:T(4,128)S(1)}, f32[3,4,256]{2,1,0:T(4,128)S(1)}, s32[1,512]{1,0:T(1,128)S(1)}, f32[16,512]{1,0:T(8,128)S(1)}, s32[1,512]{1,0...) custom-call(f32[3,4,256]{2,1,0:T(4,128)} %bitcast.6, f32[3,4,256]{2,1,0:T(4,128)} %bitcast.7, ...), custom_call_target="tpu_custom_call" | custom-call | tf_op jit(solution)/shard_map/pallas_call | solution.py:224
  1.5 0.8 %collective-permute-start = (f32[12,256]{1,0:T(8,128)S(1)}, f32[12,256]{1,0:T(8,128)S(1)}, u32[]{:S(2)}, u32[]{:S(2)}) collective-permute-start(f32[12,256]{1,0:T(8,128)S(1)} %get-tuple-element.33), channel_id=1, source_target_pairs={{0,4},{1,5},{2,6},{3,7},{4,0},{5,1},{6,2},{7,3},{8,12},{9,13},{10,... | collective-permute-start | bytes 36872 | tf_op jit(solution)/shard_map/ppermute | solution.py:245
  2.3 1.2 %collective-permute-start.1 = (f32[12,256]{1,0:T(8,128)S(1)}, f32[12,256]{1,0:T(8,128)S(1)}, u32[]{:S(2)}, u32[]{:S(2)}) collective-permute-start(f32[12,256]{1,0:T(8,128)S(1)} %get-tuple-element.34), channel_id=1, source_target_pairs={{0,1},{1,0},{2,3},{3,2},{4,8},{5,9},{6,10},{7,11},{8,4},{9,5},{10,... | collective-permute-start | bytes 36872 | tf_op jit(solution)/shard_map/ppermute | solution.py:245
  3.5 2.2 %shard_map.96 = (bf16[288,512]{1,0:T(8,128)(2,1)S(1)}, bf16[288,512]{1,0:T(8,128)(2,1)S(1)}, bf16[512,256]{1,0:T(8,128)(2,1)S(1)}, bf16[512,256]{1,0:T(8,128)(2,...) custom-call(s32[1,512]{1,0:T(1,128)S(1)} %get-tuple-element.35.sfirst_ref, ...), custom_call_target="tpu_custom_call" | custom-call | tf_op jit(solution)/shard_map/pallas_call | solution.py:224
  5.7 0.0 collective-permute-done.near_ref
  5.7 4.0 %collective-permute-done.1.far_ref = f32[12,256]{1,0:T(8,128)S(1)} collective-permute-done((f32[12,256]{1,0:T(8,128)S(1)}, f32[12,256]{1,0:T(8,128)S(1)}, u32[]{:S(2)}, u32[]{:S(2)}) %collective-permute-start.1) | collective-permute-done | bytes 12320 | tf_op jit(solution)/shard_map/ppermute | solution.py:245
  9.7 0.1 shard_map.97
  9.8 0.1 collective-permute-start.2
  9.9 0.1 collective-permute-start.4
  10.0 5.4 %collective-permute-start.3 = (f32[8,128]{1,0:T(8,128)S(1)}, f32[8,128]{1,0:T(8,128)S(1)}, u32[]{:S(2)}, u32[]{:S(2)}) collective-permute-start(f32[8,128]{1,0:T(8,128)S(1)} %get-tuple-element.45), channel_id=1, source_target_pairs={{0,4},{1,2},{2,1},{3,7},{4,0},{5,6},{6,5},{7,3},{8,12},{9,10},{10,... | collective-permute-start | bytes 12296 | tf_op jit(solution)/shard_map/ppermute | solution.py:245
  15.4 0.6 %shard_map.98 = (f32[512,128]{1,0:T(8,128)S(1)}, bf16[4,192,768]{2,1,0:T(8,128)(2,1)S(1)}, bf16[4,768,128]{2,1,0:T(8,128)(2,1)S(1)}) custom-call(f32[256,128]{1,0:T(8,128)S(1)} %get-tuple-element.38.coef_ref, bf16[512,256]{1,0:T(8,128)(2,1)S(1)} %get-tuple-element.39.high_ref, bf16[512,256]{1,0:T(8,128)(2,1)S(1)} %get-tuple-element.40.low_ref, ...), custom_call_target="tpu_custom_call" | custom-call | tf_op jit(solution)/shard_map/pallas_call | solution.py:224
  16.0 0.0 collective-permute-done.2.first_ref
  16.0 0.0 collective-permute-done.4.third_ref
  16.0 0.3 collective-permute-done.3.two_ref
  16.4 4.4 %shard_map.99 = (f32[256,128]{1,0:T(8,128)S(1)}, f32[8,128]{1,0:T(8,128)S(1)}, f32[8,128]{1,0:T(8,128)S(1)}) custom-call(f32[512,128]{1,0:T(8,128)S(1)} %get-tuple-element.43.main_ref, f32[8,128]{1,0:T(8,128)S(1)} %collective-permute-done.2.first_ref, f32[8,128]{1,0:T(8,128)S(1)} %collective-permute-done.3.two_ref, ...), custom_call_target="tpu_custom_call" | custom-call | tf_op jit(solution)/shard_map/pallas_call | solution.py:224
  20.8 0.1 collective-permute-start.5
  20.9 3.7 %collective-permute-start.6 = (f32[8,128]{1,0:T(8,128)S(1)}, f32[8,128]{1,0:T(8,128)S(1)}, u32[]{:S(2)}, u32[]{:S(2)}) collective-permute-start(f32[8,128]{1,0:T(8,128)S(1)} %get-tuple-element.54), channel_id=1, source_target_pairs={{0,4},{1,2},{2,1},{3,7},{4,0},{5,6},{6,5},{7,3},{8,12},{9,10},{10,... | collective-permute-start | bytes 12296 | tf_op jit(solution)/shard_map/ppermute | solution.py:245
  24.6 0.0 collective-permute-done.5.one_ref
  24.6 1.0 %collective-permute-done.6.two_ref = f32[8,128]{1,0:T(8,128)S(1)} collective-permute-done((f32[8,128]{1,0:T(8,128)S(1)}, f32[8,128]{1,0:T(8,128)S(1)}, u32[]{:S(2)}, u32[]{:S(2)}) %collective-permute-start.6) | collective-permute-done | bytes 4128 | tf_op jit(solution)/shard_map/ppermute | solution.py:245
  25.6 0.2 shard_map.100
  25.7 2.8 %collective-permute-start.7 = (f32[12,256]{1,0:T(8,128)S(1)}, f32[12,256]{1,0:T(8,128)S(1)}, u32[]{:S(2)}, u32[]{:S(2)}) collective-permute-start(f32[12,256]{1,0:T(8,128)S(1)} %get-tuple-element.56), channel_id=1, source_target_pairs={{0,4},{1,5},{2,6},{3,7},{4,0},{5,1},{6,2},{7,3},{8,12},{9,13},{10,... | collective-permute-start | bytes 36872 | tf_op jit(solution)/shard_map/ppermute | solution.py:245
  28.5 0.5 %collective-permute-start.8 = (f32[12,256]{1,0:T(8,128)S(1)}, f32[12,256]{1,0:T(8,128)S(1)}, u32[]{:S(2)}, u32[]{:S(2)}) collective-permute-start(f32[12,256]{1,0:T(8,128)S(1)} %get-tuple-element.57), channel_id=1, source_target_pairs={{0,1},{1,0},{2,3},{3,2},{4,8},{5,9},{6,10},{7,11},{8,4},{9,5},{10,... | collective-permute-start | bytes 36872 | tf_op jit(solution)/shard_map/ppermute | solution.py:245
  29.0 0.3 collective-permute-done.7.refs_1_
  29.4 6.5 %collective-permute-done.8.refs_2_ = f32[12,256]{1,0:T(8,128)S(1)} collective-permute-done((f32[12,256]{1,0:T(8,128)S(1)}, f32[12,256]{1,0:T(8,128)S(1)}, u32[]{:S(2)}, u32[]{:S(2)}) %collective-permute-start.8) | collective-permute-done | bytes 12320 | tf_op jit(solution)/shard_map/ppermute | solution.py:245
  35.9 0.6 %shard_map.101 = (f32[3,4,256]{2,1,0:T(4,128)}, f32[3,4,256]{2,1,0:T(4,128)}) custom-call(f32[48,256]{1,0:T(8,128)S(1)} %get-tuple-element.55.refs_0_, f32[12,256]{1,0:T(8,128)S(1)} %collective-permute-done.7.refs_1_, f32[12,256]{1,0:T(8,128)S(1)} %collective-permute-done.8.refs_2_), custom_call_target="tpu_custom_call" | custom-call | tf_op jit(solution)/shard_map/pallas_call | solution.py:224
Async XLA Ops:
  1.5 4.2 %collective-permute-start = (f32[12,256]{1,0:T(8,128)S(1)}, f32[12,256]{1,0:T(8,128)S(1)}, u32[]{:S(2)}, u32[]{:S(2)}) collective-permute-start(f32[12,256]{1,0:T(8,128)S(1)} %get-tuple-element.33), channel_id=1, source_target_pairs={{0,4},{1,5},{2,6},{3,7},{4,0},{5,1},{6,2},{7,3},{8,12},{9,13},{10,... | collective-permute-start | bytes 36872 | tf_op jit(solution)/shard_map/ppermute | solution.py:245
  2.3 7.4 %collective-permute-start.1 = (f32[12,256]{1,0:T(8,128)S(1)}, f32[12,256]{1,0:T(8,128)S(1)}, u32[]{:S(2)}, u32[]{:S(2)}) collective-permute-start(f32[12,256]{1,0:T(8,128)S(1)} %get-tuple-element.34), channel_id=1, source_target_pairs={{0,1},{1,0},{2,3},{3,2},{4,8},{5,9},{6,10},{7,11},{8,4},{9,5},{10,... | collective-permute-start | bytes 36872 | tf_op jit(solution)/shard_map/ppermute | solution.py:245
  9.8 6.2 %collective-permute-start.2 = (f32[8,128]{1,0:T(8,128)S(1)}, f32[8,128]{1,0:T(8,128)S(1)}, u32[]{:S(2)}, u32[]{:S(2)}) collective-permute-start(f32[8,128]{1,0:T(8,128)S(1)} %get-tuple-element.44), channel_id=1, source_target_pairs={{0,1},{1,0},{2,6},{3,7},{4,5},{5,4},{6,2},{7,3},{8,9},{9,8},{10,14... | collective-permute-start | bytes 12296 | tf_op jit(solution)/shard_map/ppermute | solution.py:245
  9.9 6.1 %collective-permute-start.4 = (f32[8,128]{1,0:T(8,128)S(1)}, f32[8,128]{1,0:T(8,128)S(1)}, u32[]{:S(2)}, u32[]{:S(2)}) collective-permute-start(f32[8,128]{1,0:T(8,128)S(1)} %get-tuple-element.44), channel_id=1, source_target_pairs={{0,4},{1,5},{2,3},{3,2},{4,0},{5,1},{6,7},{7,6},{8,12},{9,13},{10,... | collective-permute-start | bytes 12296 | tf_op jit(solution)/shard_map/ppermute | solution.py:245
  10.0 6.4 %collective-permute-start.3 = (f32[8,128]{1,0:T(8,128)S(1)}, f32[8,128]{1,0:T(8,128)S(1)}, u32[]{:S(2)}, u32[]{:S(2)}) collective-permute-start(f32[8,128]{1,0:T(8,128)S(1)} %get-tuple-element.45), channel_id=1, source_target_pairs={{0,4},{1,2},{2,1},{3,7},{4,0},{5,6},{6,5},{7,3},{8,12},{9,10},{10,... | collective-permute-start | bytes 12296 | tf_op jit(solution)/shard_map/ppermute | solution.py:245
  20.8 3.8 %collective-permute-start.5 = (f32[8,128]{1,0:T(8,128)S(1)}, f32[8,128]{1,0:T(8,128)S(1)}, u32[]{:S(2)}, u32[]{:S(2)}) collective-permute-start(f32[8,128]{1,0:T(8,128)S(1)} %get-tuple-element.53), channel_id=1, source_target_pairs={{0,1},{1,0},{2,3},{3,2},{4,5},{5,4},{6,7},{7,6},{8,9},{9,8},{10,11... | collective-permute-start | bytes 12296 | tf_op jit(solution)/shard_map/ppermute | solution.py:245
  20.9 4.7 %collective-permute-start.6 = (f32[8,128]{1,0:T(8,128)S(1)}, f32[8,128]{1,0:T(8,128)S(1)}, u32[]{:S(2)}, u32[]{:S(2)}) collective-permute-start(f32[8,128]{1,0:T(8,128)S(1)} %get-tuple-element.54), channel_id=1, source_target_pairs={{0,4},{1,2},{2,1},{3,7},{4,0},{5,6},{6,5},{7,3},{8,12},{9,10},{10,... | collective-permute-start | bytes 12296 | tf_op jit(solution)/shard_map/ppermute | solution.py:245
  25.7 3.6 %collective-permute-start.7 = (f32[12,256]{1,0:T(8,128)S(1)}, f32[12,256]{1,0:T(8,128)S(1)}, u32[]{:S(2)}, u32[]{:S(2)}) collective-permute-start(f32[12,256]{1,0:T(8,128)S(1)} %get-tuple-element.56), channel_id=1, source_target_pairs={{0,4},{1,5},{2,6},{3,7},{4,0},{5,1},{6,2},{7,3},{8,12},{9,13},{10,... | collective-permute-start | bytes 36872 | tf_op jit(solution)/shard_map/ppermute | solution.py:245
  28.5 7.4 %collective-permute-start.8 = (f32[12,256]{1,0:T(8,128)S(1)}, f32[12,256]{1,0:T(8,128)S(1)}, u32[]{:S(2)}, u32[]{:S(2)}) collective-permute-start(f32[12,256]{1,0:T(8,128)S(1)} %get-tuple-element.57), channel_id=1, source_target_pairs={{0,1},{1,0},{2,3},{3,2},{4,8},{5,9},{6,10},{7,11},{8,4},{9,5},{10,... | collective-permute-start | bytes 36872 | tf_op jit(solution)/shard_map/ppermute | solution.py:245

commit v6 on v5

--- a/solution.py
+++ b/solution.py
@@ -191,9 +191,10 @@
     send_two_ref[...] = jnp.where(odd, high, low)
 
 
-def turn_kernel(own_ref, one_ref, two_ref, wide_ref, near_ref, far_ref):
+def turn_kernel(own_ref, first_ref, two_ref, third_ref, wide_ref, near_ref, far_ref):
     below = parity("cell") == 1
-    one, two = unfold(one_ref[...]), unfold(two_ref[...])
+    one = jnp.where(lax.axis_index("cell") < 2, first_ref[...], third_ref[...])
+    one, two = unfold(one), unfold(two_ref[...])
     count = own_ref.shape[0]
     low = own_ref[:HS] + jnp.where(below, one, two)
     high = own_ref[count - HS :] + jnp.where(below, two, one)
@@ -267,11 +268,6 @@
         two = swap(two, two_of)
         high = swap(one, side_of(False))
         return low, two, high
-
-    def over_cell(one, two):
-        two = swap(two, two_of)
-        one = swap(one, lambda t, c: t * regions + (c ^ 1))
-        return one, two
 
     small = (jnp.swapaxes(theta, 1, 2), jnp.swapaxes(tangent, 1, 2), sfirst[None], sweight, tfirst[None], tweight)
     strip = ((12, rows), F32)
@@ -302,8 +298,8 @@
         [((rows, 128), F32), band, band],
         [pltpu.VMEM((4, cells, 768), F32), pltpu.VMEM((4, 2 * cells, 768), BF16), pltpu.VMEM((cells, 128), F32)],
     )(main, low, two, high, edge, spread, gather, shigh, slow, covariates, counts)
-    one, two = over_cell(one, two)
-    wide, near, far = call(turn_kernel, [((48, rows), F32), strip, strip])(own, one, two)
+    low, two, high = over_cell_in_three(one, two)
+    wide, near, far = call(turn_kernel, [((48, rows), F32), strip, strip])(own, low, two, high)
     near, far = over_tm(near, far)
     scales = (1.0 / (16 * (hours // 4)), 1.0 / (hours // 4))
 

time: 36.7 us -> 36.8 us (level)
    ppermute x9 -> x10, starting transfers between devices: 14.6 us -> 14.8 us  [swap(): lax.ppermute(value, ('tm', 'cell'), [(t * regions + c, partner(t, c)) for...]
    ppermute x9 -> x10, waiting for transfers between devices: 12.2 us -> 12 us  [swap(): lax.ppermute(value, ('tm', 'cell'), [(t * regions + c, partner(t, c)) for...]
  transfers between devices with their start and end apart: 9 -> 10, of which waited for: 5 -> 6; matrix products, arithmetic and copies ran while one was open for 0% -> 0% of each run, Pallas kernels for 8% -> 8%
where the time goes in v6:
time: 36.8 us; the launch traced here: 36.6 us
  starting transfers between devices  14.8 us (40%)
  waiting for transfers between devices  12 us (33%)
  Pallas kernels  9.04 us (25%)
  between operations  0.73 us (2%)
    ppermute x10, starting transfers between devices, swap(): lax.ppermute(value, ('tm', 'cell'), [(t * regions + c, partner(t, c)) for...  14.8 us
    ppermute x10, waiting for transfers between devices, swap(): lax.ppermute(value, ('tm', 'cell'), [(t * regions + c, partner(t, c)) for...  12 us
    pallas_call x7, Pallas kernels, run(): pl.pallas_call(kernel, out_shape=tuple((shape(s, d) for s, d in outs)), i...  9.04 us
  transfers between devices with their start and end apart: 10, of which 6 were waited for; matrix products, arithmetic and copies ran while one was open for 0% of the time, Pallas kernels for 8%

profile of v6, /device:TPU:95, one launch (start us, length us, event | category | flops | bytes accessed | tf_op | source)
XLA Modules:
  0.0 36.6 jit_solution(12886754140815950796)
XLA Ops:
  0.6 0.9 %shard_map.95 = (f32[3,4,256]{2,1,0:T(4,128)S(1)}, f32[3,4,256]{2,1,0:T(4,128)S(1)}, s32[1,512]{1,0:T(1,128)S(1)}, f32[16,512]{1,0:T(8,128)S(1)}, s32[1,512]{1,0...) custom-call(f32[3,4,256]{2,1,0:T(4,128)} %bitcast.6, f32[3,4,256]{2,1,0:T(4,128)} %bitcast.7, ...), custom_call_target="tpu_custom_call" | custom-call | tf_op jit(solution)/shard_map/pallas_call | solution.py:225
  1.5 0.8 %collective-permute-start = (f32[12,256]{1,0:T(8,128)S(1)}, f32[12,256]{1,0:T(8,128)S(1)}, u32[]{:S(2)}, u32[]{:S(2)}) collective-permute-start(f32[12,256]{1,0:T(8,128)S(1)} %get-tuple-element.33), channel_id=1, source_target_pairs={{0,4},{1,5},{2,6},{3,7},{4,0},{5,1},{6,2},{7,3},{8,12},{9,13},{10,... | collective-permute-start | bytes 36872 | tf_op jit(solution)/shard_map/ppermute | solution.py:246
  2.3 1.2 %collective-permute-start.1 = (f32[12,256]{1,0:T(8,128)S(1)}, f32[12,256]{1,0:T(8,128)S(1)}, u32[]{:S(2)}, u32[]{:S(2)}) collective-permute-start(f32[12,256]{1,0:T(8,128)S(1)} %get-tuple-element.34), channel_id=1, source_target_pairs={{0,1},{1,0},{2,3},{3,2},{4,8},{5,9},{6,10},{7,11},{8,4},{9,5},{10,... | collective-permute-start | bytes 36872 | tf_op jit(solution)/shard_map/ppermute | solution.py:246
  3.5 2.2 %shard_map.96 = (bf16[288,512]{1,0:T(8,128)(2,1)S(1)}, bf16[288,512]{1,0:T(8,128)(2,1)S(1)}, bf16[512,256]{1,0:T(8,128)(2,1)S(1)}, bf16[512,256]{1,0:T(8,128)(2,...) custom-call(s32[1,512]{1,0:T(1,128)S(1)} %get-tuple-element.35.sfirst_ref, ...), custom_call_target="tpu_custom_call" | custom-call | tf_op jit(solution)/shard_map/pallas_call | solution.py:225
  5.7 0.0 collective-permute-done.near_ref
  5.7 4.0 %collective-permute-done.1.far_ref = f32[12,256]{1,0:T(8,128)S(1)} collective-permute-done((f32[12,256]{1,0:T(8,128)S(1)}, f32[12,256]{1,0:T(8,128)S(1)}, u32[]{:S(2)}, u32[]{:S(2)}) %collective-permute-start.1) | collective-permute-done | bytes 12320 | tf_op jit(solution)/shard_map/ppermute | solution.py:246
  9.7 0.1 shard_map.97
  9.8 0.1 collective-permute-start.2
  9.9 0.1 collective-permute-start.4
  10.0 5.4 %collective-permute-start.3 = (f32[8,128]{1,0:T(8,128)S(1)}, f32[8,128]{1,0:T(8,128)S(1)}, u32[]{:S(2)}, u32[]{:S(2)}) collective-permute-start(f32[8,128]{1,0:T(8,128)S(1)} %get-tuple-element.45), channel_id=1, source_target_pairs={{0,4},{1,2},{2,1},{3,7},{4,0},{5,6},{6,5},{7,3},{8,12},{9,10},{10,... | collective-permute-start | bytes 12296 | tf_op jit(solution)/shard_map/ppermute | solution.py:246
  15.4 0.6 %shard_map.98 = (f32[512,128]{1,0:T(8,128)S(1)}, bf16[4,192,768]{2,1,0:T(8,128)(2,1)S(1)}, bf16[4,768,128]{2,1,0:T(8,128)(2,1)S(1)}) custom-call(f32[256,128]{1,0:T(8,128)S(1)} %get-tuple-element.38.coef_ref, bf16[512,256]{1,0:T(8,128)(2,1)S(1)} %get-tuple-element.39.high_ref, bf16[512,256]{1,0:T(8,128)(2,1)S(1)} %get-tuple-element.40.low_ref, ...), custom_call_target="tpu_custom_call" | custom-call | tf_op jit(solution)/shard_map/pallas_call | solution.py:225
  16.0 0.0 collective-permute-done.2.first_ref
  16.0 0.0 collective-permute-done.4.third_ref
  16.0 0.3 collective-permute-done.3.two_ref
  16.4 4.4 %shard_map.99 = (f32[256,128]{1,0:T(8,128)S(1)}, f32[8,128]{1,0:T(8,128)S(1)}, f32[8,128]{1,0:T(8,128)S(1)}) custom-call(f32[512,128]{1,0:T(8,128)S(1)} %get-tuple-element.43.main_ref, f32[8,128]{1,0:T(8,128)S(1)} %collective-permute-done.2.first_ref, f32[8,128]{1,0:T(8,128)S(1)} %collective-permute-done.3.two_ref, ...), custom_call_target="tpu_custom_call" | custom-call | tf_op jit(solution)/shard_map/pallas_call | solution.py:225
  20.8 0.1 collective-permute-start.5
  20.9 5.4 %collective-permute-start.6 = (f32[8,128]{1,0:T(8,128)S(1)}, f32[8,128]{1,0:T(8,128)S(1)}, u32[]{:S(2)}, u32[]{:S(2)}) collective-permute-start(f32[8,128]{1,0:T(8,128)S(1)} %get-tuple-element.54), channel_id=1, source_target_pairs={{0,4},{1,2},{2,1},{3,7},{4,0},{5,6},{6,5},{7,3},{8,12},{9,10},{10,... | collective-permute-start | bytes 12296 | tf_op jit(solution)/shard_map/ppermute | solution.py:246
  26.3 0.4 %collective-permute-start.7 = (f32[8,128]{1,0:T(8,128)S(1)}, f32[8,128]{1,0:T(8,128)S(1)}, u32[]{:S(2)}, u32[]{:S(2)}) collective-permute-start(f32[8,128]{1,0:T(8,128)S(1)} %get-tuple-element.53), channel_id=1, source_target_pairs={{0,4},{1,5},{2,3},{3,2},{4,0},{5,1},{6,7},{7,6},{8,12},{9,13},{10,... | collective-permute-start | bytes 12296 | tf_op jit(solution)/shard_map/ppermute | solution.py:246
  26.7 0.0 collective-permute-done.5.first_ref
  26.7 0.6 %collective-permute-done.6.two_ref = f32[8,128]{1,0:T(8,128)S(1)} collective-permute-done((f32[8,128]{1,0:T(8,128)S(1)}, f32[8,128]{1,0:T(8,128)S(1)}, u32[]{:S(2)}, u32[]{:S(2)}) %collective-permute-start.6) | collective-permute-done | bytes 4128 | tf_op jit(solution)/shard_map/ppermute | solution.py:246
  27.3 0.2 collective-permute-done.7.third_ref
  27.5 0.2 shard_map.100
  27.7 0.9 %collective-permute-start.8 = (f32[12,256]{1,0:T(8,128)S(1)}, f32[12,256]{1,0:T(8,128)S(1)}, u32[]{:S(2)}, u32[]{:S(2)}) collective-permute-start(f32[12,256]{1,0:T(8,128)S(1)} %get-tuple-element.56), channel_id=1, source_target_pairs={{0,4},{1,5},{2,6},{3,7},{4,0},{5,1},{6,2},{7,3},{8,12},{9,13},{10,... | collective-permute-start | bytes 36872 | tf_op jit(solution)/shard_map/ppermute | solution.py:246
  28.5 0.5 %collective-permute-start.9 = (f32[12,256]{1,0:T(8,128)S(1)}, f32[12,256]{1,0:T(8,128)S(1)}, u32[]{:S(2)}, u32[]{:S(2)}) collective-permute-start(f32[12,256]{1,0:T(8,128)S(1)} %get-tuple-element.57), channel_id=1, source_target_pairs={{0,1},{1,0},{2,3},{3,2},{4,8},{5,9},{6,10},{7,11},{8,4},{9,5},{10,... | collective-permute-start | bytes 36872 | tf_op jit(solution)/shard_map/ppermute | solution.py:246
  29.0 0.3 collective-permute-done.8.refs_1_
  29.4 6.5 %collective-permute-done.9.refs_2_ = f32[12,256]{1,0:T(8,128)S(1)} collective-permute-done((f32[12,256]{1,0:T(8,128)S(1)}, f32[12,256]{1,0:T(8,128)S(1)}, u32[]{:S(2)}, u32[]{:S(2)}) %collective-permute-start.9) | collective-permute-done | bytes 12320 | tf_op jit(solution)/shard_map/ppermute | solution.py:246
  35.9 0.6 %shard_map.101 = (f32[3,4,256]{2,1,0:T(4,128)}, f32[3,4,256]{2,1,0:T(4,128)}) custom-call(f32[48,256]{1,0:T(8,128)S(1)} %get-tuple-element.55.refs_0_, f32[12,256]{1,0:T(8,128)S(1)} %collective-permute-done.8.refs_1_, f32[12,256]{1,0:T(8,128)S(1)} %collective-permute-done.9.refs_2_), custom_call_target="tpu_custom_call" | custom-call | tf_op jit(solution)/shard_map/pallas_call | solution.py:225
Async XLA Ops:
  1.5 4.2 %collective-permute-start = (f32[12,256]{1,0:T(8,128)S(1)}, f32[12,256]{1,0:T(8,128)S(1)}, u32[]{:S(2)}, u32[]{:S(2)}) collective-permute-start(f32[12,256]{1,0:T(8,128)S(1)} %get-tuple-element.33), channel_id=1, source_target_pairs={{0,4},{1,5},{2,6},{3,7},{4,0},{5,1},{6,2},{7,3},{8,12},{9,13},{10,... | collective-permute-start | bytes 36872 | tf_op jit(solution)/shard_map/ppermute | solution.py:246
  2.3 7.4 %collective-permute-start.1 = (f32[12,256]{1,0:T(8,128)S(1)}, f32[12,256]{1,0:T(8,128)S(1)}, u32[]{:S(2)}, u32[]{:S(2)}) collective-permute-start(f32[12,256]{1,0:T(8,128)S(1)} %get-tuple-element.34), channel_id=1, source_target_pairs={{0,1},{1,0},{2,3},{3,2},{4,8},{5,9},{6,10},{7,11},{8,4},{9,5},{10,... | collective-permute-start | bytes 36872 | tf_op jit(solution)/shard_map/ppermute | solution.py:246
  9.8 6.2 %collective-permute-start.2 = (f32[8,128]{1,0:T(8,128)S(1)}, f32[8,128]{1,0:T(8,128)S(1)}, u32[]{:S(2)}, u32[]{:S(2)}) collective-permute-start(f32[8,128]{1,0:T(8,128)S(1)} %get-tuple-element.44), channel_id=1, source_target_pairs={{0,1},{1,0},{2,6},{3,7},{4,5},{5,4},{6,2},{7,3},{8,9},{9,8},{10,14... | collective-permute-start | bytes 12296 | tf_op jit(solution)/shard_map/ppermute | solution.py:246
  9.9 6.1 %collective-permute-start.4 = (f32[8,128]{1,0:T(8,128)S(1)}, f32[8,128]{1,0:T(8,128)S(1)}, u32[]{:S(2)}, u32[]{:S(2)}) collective-permute-start(f32[8,128]{1,0:T(8,128)S(1)} %get-tuple-element.44), channel_id=1, source_target_pairs={{0,4},{1,5},{2,3},{3,2},{4,0},{5,1},{6,7},{7,6},{8,12},{9,13},{10,... | collective-permute-start | bytes 12296 | tf_op jit(solution)/shard_map/ppermute | solution.py:246
  10.0 6.4 %collective-permute-start.3 = (f32[8,128]{1,0:T(8,128)S(1)}, f32[8,128]{1,0:T(8,128)S(1)}, u32[]{:S(2)}, u32[]{:S(2)}) collective-permute-start(f32[8,128]{1,0:T(8,128)S(1)} %get-tuple-element.45), channel_id=1, source_target_pairs={{0,4},{1,2},{2,1},{3,7},{4,0},{5,6},{6,5},{7,3},{8,12},{9,10},{10,... | collective-permute-start | bytes 12296 | tf_op jit(solution)/shard_map/ppermute | solution.py:246
  20.8 5.9 %collective-permute-start.5 = (f32[8,128]{1,0:T(8,128)S(1)}, f32[8,128]{1,0:T(8,128)S(1)}, u32[]{:S(2)}, u32[]{:S(2)}) collective-permute-start(f32[8,128]{1,0:T(8,128)S(1)} %get-tuple-element.53), channel_id=1, source_target_pairs={{0,1},{1,0},{2,6},{3,7},{4,5},{5,4},{6,2},{7,3},{8,9},{9,8},{10,14... | collective-permute-start | bytes 12296 | tf_op jit(solution)/shard_map/ppermute | solution.py:246
  20.9 6.4 %collective-permute-start.6 = (f32[8,128]{1,0:T(8,128)S(1)}, f32[8,128]{1,0:T(8,128)S(1)}, u32[]{:S(2)}, u32[]{:S(2)}) collective-permute-start(f32[8,128]{1,0:T(8,128)S(1)} %get-tuple-element.54), channel_id=1, source_target_pairs={{0,4},{1,2},{2,1},{3,7},{4,0},{5,6},{6,5},{7,3},{8,12},{9,10},{10,... | collective-permute-start | bytes 12296 | tf_op jit(solution)/shard_map/ppermute | solution.py:246
  26.3 1.2 %collective-permute-start.7 = (f32[8,128]{1,0:T(8,128)S(1)}, f32[8,128]{1,0:T(8,128)S(1)}, u32[]{:S(2)}, u32[]{:S(2)}) collective-permute-start(f32[8,128]{1,0:T(8,128)S(1)} %get-tuple-element.53), channel_id=1, source_target_pairs={{0,4},{1,5},{2,3},{3,2},{4,0},{5,1},{6,7},{7,6},{8,12},{9,13},{10,... | collective-permute-start | bytes 12296 | tf_op jit(solution)/shard_map/ppermute | solution.py:246
  27.7 1.7 %collective-permute-start.8 = (f32[12,256]{1,0:T(8,128)S(1)}, f32[12,256]{1,0:T(8,128)S(1)}, u32[]{:S(2)}, u32[]{:S(2)}) collective-permute-start(f32[12,256]{1,0:T(8,128)S(1)} %get-tuple-element.56), channel_id=1, source_target_pairs={{0,4},{1,5},{2,6},{3,7},{4,0},{5,1},{6,2},{7,3},{8,12},{9,13},{10,... | collective-permute-start | bytes 36872 | tf_op jit(solution)/shard_map/ppermute | solution.py:246
  28.5 7.4 %collective-permute-start.9 = (f32[12,256]{1,0:T(8,128)S(1)}, f32[12,256]{1,0:T(8,128)S(1)}, u32[]{:S(2)}, u32[]{:S(2)}) collective-permute-start(f32[12,256]{1,0:T(8,128)S(1)} %get-tuple-element.57), channel_id=1, source_target_pairs={{0,1},{1,0},{2,3},{3,2},{4,8},{5,9},{6,10},{7,11},{8,4},{9,5},{10,... | collective-permute-start | bytes 36872 | tf_op jit(solution)/shard_map/ppermute | solution.py:246
